TPU v7x, 512 devices: a whole 4x8x8 slice. The times are simulated.
512 devices in a mesh: grp: 8 (over z), slab: 64 (over y, x, core).
Axes of the slice: x: 4, y: 8, z: 8, core: 2. Of those that a mesh axis runs over, the one named last changes fastest.
Arguments:
- thermal_state_values: float32 [1024, 512], P(('grp', 'slab')), may hold values from -6 to 6
- thermal_kappa_values: float32 [512, 128], P(('grp', 'slab')), may hold values from 0.5 to 2
- nodal_heating_input: float32 [1024, 512], P(('grp', 'slab')), may hold values from -24 to 24
- frozen_share_map: float32 [4096, 8192], P('grp', 'slab'), may hold values from 0 to 1
- crystal_label_map: int32 [4096, 8192], P('grp', 'slab'), may hold values from 0 to 7999
- growth_reach_table: int32 [8000, 6], replicated, may hold values from 1 to 4
- seed_site_slots: int32 [131072], P(('grp', 'slab')), may hold values from 0 to 65535
- seed_crystal_label: int32 [131072], P(('grp', 'slab')), may hold values from 0 to 7999
Outputs:
- new_temperature: float32 [1024, 512], P(('grp', 'slab'))
- new_solid: float32 [4096, 8192], P('grp', 'slab')
Inputs may be any that keep to these rules, and one draw needn't show every extreme that they name: `seed_site_slots`: each entry is a cell of the brick of the device that holds the entry, numbered x * 8 * 16 + y * 16 + z in that brick's own coordinates; entries may repeat.
All inputs are finite; a program needn't handle non-finite values.
Results may differ from a plain program's by a relative error of at most 0.0001.
Values sent between devices are 32-bit elements; how exact they have to be, the bound alone decides.
A program may use at most 128 MiB of HBM per device.

v0:
```python
import jax
import jax.numpy as jnp
from jax import lax
from jax.sharding import PartitionSpec as P

HEX_COUNT_LATER = 2
CPC = 8


HIGHEST = lax.Precision.HIGHEST
step_size = 0.004
DERIVS = ((-3.0, 4.0, -1.0), (-1.0, 0.0, 1.0), (1.0, -4.0, 3.0))
WEIGHTS = (1.0 / 6.0, 2.0 / 3.0, 1.0 / 6.0)


def passed_along(array, axis, by):
    count = lax.axis_size(axis)
    return lax.ppermute(array, axis, [(i, (i + by) % count) for i in range(count)])


def extended_2(array, sides, width):
    for axis, dim in sides:
        count, length = (lax.axis_size(axis), array.shape[dim])
        up = [(i, (i + 1) % count) for i in range(count)]
        down = [(j, i) for i, j in up]
        last = lax.slice_in_dim(array, length - width, length, axis=dim)
        first = lax.slice_in_dim(array, 0, width, axis=dim)
        before = lax.ppermute(last, axis, up)
        after = lax.ppermute(first, axis, down)
        array = jnp.concatenate([before, array, after], axis=dim)
    return array


def alternate(even_part, odd_part, which_axis):
    stacked = jnp.stack([even_part, odd_part], which_axis + 1)
    shape = list(even_part.shape)
    shape[which_axis] = 2 * shape[which_axis]
    return stacked.reshape(shape)


def spread_periodic(values, which_axis):
    even_part = WEIGHTS[0] * values + WEIGHTS[2] * jnp.roll(values, 1, which_axis)
    return alternate(even_part, WEIGHTS[1] * values, which_axis)


def spread_open(values, which_axis):
    count = values.shape[which_axis]
    zero_plane = jnp.zeros_like(values)
    even_part = WEIGHTS[0] * jnp.concatenate([values, zero_plane], which_axis) + WEIGHTS[
        2
    ] * jnp.concatenate([zero_plane, values], which_axis)
    paired = alternate(
        lax.slice_in_dim(even_part, 0, count, 1, which_axis), WEIGHTS[1] * values, which_axis
    )
    return jnp.concatenate(
        [paired, lax.slice_in_dim(even_part, count, count + 1, 1, which_axis)], which_axis
    )


def place_even(values, which_axis):
    return alternate(values, jnp.zeros_like(values), which_axis)


def coefficients(kappa, rows_y):
    layers = kappa.shape[0]
    cube = kappa.reshape(layers, rows_y, -1)
    along_x = spread_periodic(spread_periodic(cube, 1), 2).reshape(layers, -1)
    along_y = spread_periodic(place_even(spread_open(cube, 0), 1), 2).reshape(2 * layers + 1, -1)
    along_z = place_even(spread_periodic(spread_open(cube, 0), 1), 2).reshape(2 * layers + 1, -1)
    return (along_x, along_y, along_z)


def contract(first, second, third, coefficient):
    terms = []
    for point in range(3):
        slope = DERIVS[point][0] * first + DERIVS[point][1] * second + DERIVS[point][2] * third
        terms.append(WEIGHTS[point] * coefficient * slope)
    results = []
    for local in range(3):
        results.append(
            DERIVS[0][local] * terms[0] + DERIVS[1][local] * terms[1] + DERIVS[2][local] * terms[2]
        )
    return results


def local_action(extended, coeff_set, plane_width):
    along_x, along_y, along_z = coeff_set
    layers = along_x.shape[0]
    flat = extended.shape[1]
    first = extended[0 : 2 * layers : 2]
    second = extended[1 : 2 * layers : 2]
    third = extended[2 : 2 * layers + 1 : 2]
    parts = contract(first, second, third, along_x)
    zero_plane = jnp.zeros((1, flat), jnp.float32)
    even_part = jnp.concatenate([parts[0], zero_plane], 0) + jnp.concatenate(
        [zero_plane, parts[2]], 0
    )
    result = jnp.concatenate([alternate(even_part[:layers], parts[1], 0), even_part[layers:]], 0)
    parts = contract(
        extended,
        jnp.roll(extended, -plane_width, 1),
        jnp.roll(extended, -2 * plane_width, 1),
        along_y,
    )
    result = (
        result
        + parts[0]
        + jnp.roll(parts[1], plane_width, 1)
        + jnp.roll(parts[2], 2 * plane_width, 1)
    )
    z_index = jnp.arange(flat) % plane_width
    ahead_two = jnp.where(
        z_index == plane_width - 2,
        jnp.roll(extended, plane_width - 2, 1),
        jnp.roll(extended, -2, 1),
    )
    parts = contract(extended, jnp.roll(extended, -1, 1), ahead_two, along_z)
    behind_two = jnp.where(
        z_index == 0, jnp.roll(parts[2], 2 - plane_width, 1), jnp.roll(parts[2], 2, 1)
    )
    return result + parts[0] + jnp.roll(parts[1], 1, 1) + behind_two


def node_mass(length):
    return jnp.where(jnp.arange(length) % 2 == 0, 1.0 / 3.0, 2.0 / 3.0).astype(jnp.float32)


def basis_columns():
    points = (jnp.arange(CPC, dtype=jnp.float32) + 0.5) / CPC
    return jnp.stack(
        [
            2.0 * (points - 0.5) * (points - 1.0),
            -4.0 * points * (points - 1.0),
            2.0 * points * (points - 0.5),
        ],
        axis=1,
    )


def element_matrix(count, node_count):
    columns = basis_columns()
    cell = jnp.arange(count * CPC)
    element = cell // CPC
    within = cell % CPC
    node = jnp.arange(node_count)[:, None]
    matrix = jnp.zeros((node_count, count * CPC), jnp.float32)
    for local in range(3):
        matrix = matrix + jnp.where(
            node == (2 * element[None, :] + local) % node_count,
            columns[within, local][None, :],
            0.0,
        )
    return matrix


def interp_rows(tensor, matrix_y, matrix_z):
    row_count, node_rows, plane_width = tensor.shape
    deep = jnp.dot(
        tensor.reshape(row_count * node_rows, plane_width), matrix_z, precision=HIGHEST
    ).reshape(row_count, node_rows, -1)
    result = jnp.einsum("rqz,qy->ryz", deep, matrix_y, precision=HIGHEST)
    return result.reshape(row_count, -1)


def next_plane(values):
    return passed_along(values[:1], ("grp", "slab"), -1)


def body(
    thermal_state_values,
    thermal_kappa_values,
    nodal_heating_input,
    frozen_share_map,
    crystal_label_map,
    growth_reach_table,
    seed_site_slots,
    seed_crystal_label,
):
    layers = thermal_kappa_values.shape[0]
    rows_y = thermal_kappa_values.shape[1] // HEX_COUNT_LATER
    plane_width = 2 * HEX_COUNT_LATER
    depth = CPC * HEX_COUNT_LATER
    flat_nodes = thermal_state_values.shape[1]
    mass_plane = (node_mass(2 * rows_y)[:, None] * node_mass(plane_width)[None, :]).reshape(
        1, flat_nodes
    )
    lumped_mass = node_mass(2 * layers)[:, None] * mass_plane
    coeff_set = coefficients(thermal_kappa_values, rows_y)

    def operate(values):
        upper_plane = next_plane(values)
        acted = local_action(jnp.concatenate([values, upper_plane], 0), coeff_set, plane_width)
        back_plane = passed_along(acted[2 * layers :], ("grp", "slab"), 1)
        return jnp.concatenate([acted[:1] + back_plane, acted[1 : 2 * layers]], 0)

    rate_one = (nodal_heating_input - operate(thermal_state_values)) / lumped_mass
    middle = thermal_state_values + step_size * rate_one
    rate_two = (nodal_heating_input - operate(middle)) / lumped_mass
    new_field = thermal_state_values + 0.5 * step_size * (rate_one + rate_two)
    extended = jnp.concatenate([new_field, next_plane(new_field)], 0)
    matrix_x = element_matrix(layers, 2 * layers + 1).T
    matrix_z = element_matrix(HEX_COUNT_LATER, plane_width)
    planes_x = jnp.dot(matrix_x, extended, precision=HIGHEST)
    slab_cells = interp_rows(
        planes_x.reshape(layers * CPC, 2 * rows_y, plane_width),
        element_matrix(rows_y, 2 * rows_y),
        matrix_z,
    )
    cell_temp = lax.all_to_all(slab_cells, "slab", split_axis=1, concat_axis=0, tiled=True)
    edge_x = frozen_share_map.shape[0]
    flat_cells = frozen_share_map.shape[1]
    edge_y = flat_cells // depth
    level_table = growth_reach_table.T.astype(jnp.float32) / 4.0
    weighted = jnp.take(level_table, crystal_label_map, axis=1) * frozen_share_map[None]
    quarter = jnp.transpose(weighted[:4].reshape(4, edge_x, edge_y, depth), (0, 2, 3, 1))
    padded = extended_2(quarter, (("grp", 3), ("slab", 1)), 1)
    sideways = (
        padded[0, 1:-1, :, 2:]
        + padded[1, 1:-1, :, :-2]
        + padded[2, 2:, :, 1:-1]
        + padded[3, :-2, :, 1:-1]
    )
    gathered = jnp.transpose(sideways, (2, 0, 1)).reshape(edge_x, flat_cells)
    depth_index = jnp.arange(flat_cells) % depth
    gathered = gathered + jnp.where(
        depth_index == depth - 1, jnp.roll(weighted[4], depth - 1, 1), jnp.roll(weighted[4], -1, 1)
    )
    gathered = gathered + jnp.where(
        depth_index == 0, jnp.roll(weighted[5], 1 - depth, 1), jnp.roll(weighted[5], 1, 1)
    )
    mean_level = jnp.sum(growth_reach_table.astype(jnp.float32), axis=1) / 6.0
    site_value = jnp.take(mean_level, seed_crystal_label)
    nucleation = (
        jnp.zeros((edge_x * flat_cells,), jnp.float32)
        .at[seed_site_slots]
        .add(site_value)
        .reshape(edge_x, flat_cells)
    )
    undercool = jnp.maximum(-cell_temp, 0.0)
    capture_rate = undercool * undercool * gathered + undercool * nucleation
    new_solid = frozen_share_map + (1.0 - frozen_share_map) * (1.0 - jnp.exp(-capture_rate))
    return (new_field, new_solid)


def solution(mesh):
    in_specs = (
        P(("grp", "slab"), None),
        P(("grp", "slab"), None),
        P(("grp", "slab"), None),
        P("grp", "slab"),
        P("grp", "slab"),
        P(),
        P(("grp", "slab")),
        P(("grp", "slab")),
    )
    out_specs = (P(("grp", "slab"), None), P("grp", "slab"))
    return jax.shard_map(body, mesh=mesh, in_specs=in_specs, out_specs=out_specs, check_vma=False)
```

profile of v0, /device:TPU:1, one launch (start us, length us, event | category | flops | bytes accessed | tf_op | source)
XLA Modules:
  0.0 351.7 jit_solution(7214582248105680628)
XLA Ops:
  0.6 0.7 slice.302
  1.3 8.7 %collective-permute-start = (f32[1,512]{1,0:T(1,128)S(1)}, f32[1,512]{1,0:T(1,128)S(1)}, u32[]{:S(2)}, u32[]{:S(2)}) collective-permute-start(f32[1,512]{1,0:T(1,128)S(1)} %slice.302), channel_id=1, source_target_pairs={{0,511},{1,0},{2,1},{3,2},{4,3},{5,4},{6,5},{7,6},{8,7},{9,8},{10,... | collective-permute-start | bytes 6152 | tf_op jit(solution)/shard_map/ppermute | solution.py:18
  10.1 1.0 bitcast_clamp_fusion
  11.1 1.0 compare_and_fusion
  12.1 1.0 convert_reduce_fusion
  13.2 3.1 copy.200
  16.2 219.2 %gather_fusion.9 = f32[65536,6]{1,0:T(8,128)} fusion(f32[6,8000]{0,1:T(8,128)} %copy.200, s32[65536]{0:T(1024)S(1)} %bitcast_clamp_fusion), kind=kCustom, calls=%fused_computation.9 | custom fusion | bytes 3407872 | tf_op jit(solution)/shard_map/jit(_take)/gather | solution.py:214
  235.4 18.2 %copy.201 = f32[512,128,6]{1,0,2:T(8,128)S(1)} copy(f32[512,128,6]{2,1,0:T(8,128)} %bitcast.137) | data formatting | bytes 3145728 | tf_op jit(solution)/shard_map/jit(_take)/gather | solution.py:214
  253.7 1.1 slice.487
  254.8 1.6 copy.202
  256.4 0.9 fusion.135
  257.2 5.3 %collective-permute-start.5 = (f32[4,8,16,1]{3,2,1,0:T(8,128)}, f32[4,8,16,1]{3,2,1,0:T(8,128)}, u32[]{:S(2)}, u32[]{:S(2)}) collective-permute-start(f32[4,8,16,1]{3,2,1,0:T(8,128)} %get-tuple-element.38), channel_id=1, source_target_pairs={{64,0},{128,64},{192,128},{256,192},{320,256},{384,320},{448,384},... | collective-permute-start | bytes 6152 | tf_op jit(solution)/shard_map/ppermute | solution.py:29
  262.5 1.9 collective-permute-start.6
  264.5 0.5 broadcast.1578
  265.0 0.7 fusion.134
  266.5 0.7 slice_bitcast_fusion
  269.5 0.2 stack_reshape.3
  269.8 0.2 mul.794
  270.1 0.2 mul.790
  270.2 0.2 reshape.794
  270.5 1.7 gather_fusion.10
  272.4 0.2 copy.179
  272.6 0.2 mul.766
  272.8 0.2 copy.180
  273.0 0.2 mul.773
  273.2 0.2 copy.194
  273.4 0.5 mul.821
  273.9 0.2 copy.195
  274.1 0.5 mul.827
  274.6 0.2 copy.187
  274.9 0.5 mul.796
  275.4 0.2 copy.188
  275.6 0.5 mul.803
  277.2 3.3 collective-permute-start.1
  280.6 6.0 %collective-permute-done.1 = f32[1,512]{1,0:T(1,128)S(1)} collective-permute-done((f32[1,512]{1,0:T(1,128)S(1)}, f32[1,512]{1,0:T(1,128)S(1)}, u32[]{:S(2)}, u32[]{:S(2)}) %collective-permute-start.1) | collective-permute-done | bytes 2080 | tf_op jit(solution)/shard_map/ppermute | solution.py:18
  286.7 9.7 %collective-permute-start.2 = (f32[1,512]{1,0:T(1,128)S(1)}, f32[1,512]{1,0:T(1,128)S(1)}, u32[]{:S(2)}, u32[]{:S(2)}) collective-permute-start(f32[1,512]{1,0:T(1,128)S(1)} %slice.449), channel_id=1, source_target_pairs={{0,511},{1,0},{2,1},{3,2},{4,3},{5,4},{6,5},{7,6},{8,7},{9,8},{10,... | collective-permute-start | bytes 6152 | tf_op jit(solution)/shard_map/ppermute | solution.py:18
  296.4 0.8 collective-permute-done.2
  298.3 1.9 collective-permute-start.3
  300.2 1.1 collective-permute-done.3
  301.4 9.7 %collective-permute-start.4 = (f32[1,512]{1,0:T(1,128)S(1)}, f32[1,512]{1,0:T(1,128)S(1)}, u32[]{:S(2)}, u32[]{:S(2)}) collective-permute-start(f32[1,512]{1,0:T(1,128)S(1)} %slice.486), channel_id=1, source_target_pairs={{0,511},{1,0},{2,1},{3,2},{4,3},{5,4},{6,5},{7,6},{8,7},{9,8},{10,... | collective-permute-start | bytes 6152 | tf_op jit(solution)/shard_map/ppermute | solution.py:18
  311.2 0.6 gather_fusion.5
  311.8 0.6 gather_fusion.4
  312.4 0.6 gather_fusion.3
  313.1 0.6 gather_fusion.8
  313.7 0.6 gather_fusion.7
  314.4 0.6 gather_fusion.6
  315.0 2.6 gather_fusion.2
  317.7 2.6 gather_fusion.1
  320.3 2.6 gather_fusion
  323.0 0.6 fusion.47
  323.7 0.3 fusion.81
  324.0 1.2 fusion.12
  325.2 1.5 copy.198
  326.7 1.3 all_to_all.10
  328.0 1.9 copy.199
  329.9 4.4 %all-to-all-start = ((f32[8,64,128]{2,0,1:T(8,128)}), f32[8,64,128]{2,0,1:T(8,128)S(1)}, u32[]{:S(2)}, u32[]{:S(2)}) async-start(f32[8,64,128]{2,0,1:T(8,128)} %copy.199), calls=%async_computation | async-start | bytes 524288 | tf_op jit(solution)/shard_map/all_to_all | solution.py:209
  334.3 1.7 pad_maximum_fusion.10
  336.0 3.4 collective-permute-start.8
  339.4 1.9 collective-permute-start.7
  341.9 2.0 scatter_custom_fusion
  344.0 2.7 collective-permute-done.7
  346.7 1.9 fusion
  348.6 1.1 copy.203
  349.7 2.0 fusion.11
  (152 shorter events, 6.5 us)
Async XLA Ops:
  1.3 274.8 %collective-permute-start = (f32[1,512]{1,0:T(1,128)S(1)}, f32[1,512]{1,0:T(1,128)S(1)}, u32[]{:S(2)}, u32[]{:S(2)}) collective-permute-start(f32[1,512]{1,0:T(1,128)S(1)} %slice.302), channel_id=1, source_target_pairs={{0,511},{1,0},{2,1},{3,2},{4,3},{5,4},{6,5},{7,6},{8,7},{9,8},{10,... | collective-permute-start | bytes 6152 | tf_op jit(solution)/shard_map/ppermute | solution.py:18
  235.4 18.2 %copy-start.1 = (f32[512,128]{1,0:T(8,128)S(1)}, f32[512,128]{1,0:T(8,128)}, u32[]{:S(2)}) copy-start(f32[512,128]{1,0:T(8,128)} %param.11) | copy-start | bytes 786436
  254.8 10.2 %copy-start.7 = (f32[1,128]{1,0:T(1,128)S(1)}, f32[1,128]{1,0:T(1,128)}, u32[]{:S(2)}) copy-start(f32[1,128]{1,0:T(1,128)} %param.9) | copy-start | bytes 1540
  257.2 77.0 %collective-permute-start.5 = (f32[4,8,16,1]{3,2,1,0:T(8,128)}, f32[4,8,16,1]{3,2,1,0:T(8,128)}, u32[]{:S(2)}, u32[]{:S(2)}) collective-permute-start(f32[4,8,16,1]{3,2,1,0:T(8,128)} %get-tuple-element.38), channel_id=1, source_target_pairs={{64,0},{128,64},{192,128},{256,192},{320,256},{384,320},{448,384},... | collective-permute-start | bytes 6152 | tf_op jit(solution)/shard_map/ppermute | solution.py:29
  262.5 71.7 %collective-permute-start.6 = (f32[4,8,16,1]{3,2,1,0:T(8,128)}, f32[4,8,16,1]{3,2,1,0:T(8,128)}, u32[]{:S(2)}, u32[]{:S(2)}) collective-permute-start(f32[4,8,16,1]{3,2,1,0:T(8,128)} %get-tuple-element.37), channel_id=1, source_target_pairs={{0,64},{64,128},{128,192},{192,256},{256,320},{320,384},{384,448},... | collective-permute-start | bytes 6152 | tf_op jit(solution)/shard_map/ppermute | solution.py:28
  266.5 3.9 %copy-start.5 = (s32[256]{0:T(256)S(1)}, s32[256]{0:T(256)}, u32[]{:S(2)}) copy-start(s32[256]{0:T(256)} %param.15) | copy-start | bytes 3076
  273.2 3.0 copy-start.2
  273.9 12.7 %copy-start.4 = (f32[2,512]{1,0:T(2,128)S(1)}, f32[2,512]{1,0:T(2,128)}, u32[]{:S(2)}) copy-start(f32[2,512]{1,0:T(2,128)} %param.10) | copy-start | bytes 12292
  277.2 9.4 %collective-permute-start.1 = (f32[1,512]{1,0:T(1,128)S(1)}, f32[1,512]{1,0:T(1,128)S(1)}, u32[]{:S(2)}, u32[]{:S(2)}) collective-permute-start(f32[1,512]{1,0:T(1,128)S(1)} %slice.447), channel_id=1, source_target_pairs={{0,1},{1,2},{2,3},{3,4},{4,5},{5,6},{6,7},{7,8},{8,9},{9,10},{10,1... | collective-permute-start | bytes 6152 | tf_op jit(solution)/shard_map/ppermute | solution.py:18
  286.7 10.5 %collective-permute-start.2 = (f32[1,512]{1,0:T(1,128)S(1)}, f32[1,512]{1,0:T(1,128)S(1)}, u32[]{:S(2)}, u32[]{:S(2)}) collective-permute-start(f32[1,512]{1,0:T(1,128)S(1)} %slice.449), channel_id=1, source_target_pairs={{0,511},{1,0},{2,1},{3,2},{4,3},{5,4},{6,5},{7,6},{8,7},{9,8},{10,... | collective-permute-start | bytes 6152 | tf_op jit(solution)/shard_map/ppermute | solution.py:18
  298.3 3.1 collective-permute-start.3
  301.4 21.5 %copy-start.3 = (f32[2,512]{1,0:T(2,128)}, f32[2,512]{1,0:T(2,128)S(1)}, u32[]{:S(2)}) copy-start(f32[2,512]{1,0:T(2,128)S(1)} %multiply_add_fusion.8) | copy-start | bytes 12292
  301.4 21.5 %collective-permute-start.4 = (f32[1,512]{1,0:T(1,128)S(1)}, f32[1,512]{1,0:T(1,128)S(1)}, u32[]{:S(2)}, u32[]{:S(2)}) collective-permute-start(f32[1,512]{1,0:T(1,128)S(1)} %slice.486), channel_id=1, source_target_pairs={{0,511},{1,0},{2,1},{3,2},{4,3},{5,4},{6,5},{7,6},{8,7},{9,8},{10,... | collective-permute-start | bytes 6152 | tf_op jit(solution)/shard_map/ppermute | solution.py:18
  328.0 13.3 %copy-start.6 = (s32[256]{0:T(256)S(1)}, s32[256]{0:T(256)}, u32[]{:S(2)}) copy-start(s32[256]{0:T(256)} %param.14) | copy-start | bytes 3076
  328.0 13.3 %copy-start = (f32[512,128]{1,0:T(8,128)S(1)}, f32[512,128]{1,0:T(8,128)}, u32[]{:S(2)}) copy-start(f32[512,128]{1,0:T(8,128)} %get-tuple-element.34) | copy-start | bytes 786436
  329.9 19.8 %all-to-all-start = ((f32[8,64,128]{2,0,1:T(8,128)}), f32[8,64,128]{2,0,1:T(8,128)S(1)}, u32[]{:S(2)}, u32[]{:S(2)}) async-start(f32[8,64,128]{2,0,1:T(8,128)} %copy.199), calls=%async_computation | async-start | bytes 524288 | tf_op jit(solution)/shard_map/all_to_all | solution.py:209
  336.0 8.0 %collective-permute-start.8 = (f32[4,1,16,514]{3,2,1,0:T(8,128)}, f32[4,1,16,514]{3,2,1,0:T(8,128)S(1)}, u32[]{:S(2)}, u32[]{:S(2)}) collective-permute-start(f32[4,1,16,514]{3,2,1,0:T(8,128)} %get-tuple-element.36), channel_id=1, source_target_pairs={{0,1},{1,2},{2,3},{3,4},{4,5},{5,6},{6,7},{7,8},{8,9},{9,10},{10,1... | collective-permute-start | bytes 394760 | tf_op jit(solution)/shard_map/ppermute | solution.py:28
  339.4 7.3 %collective-permute-start.7 = (f32[4,1,16,514]{3,2,1,0:T(8,128)}, f32[4,1,16,514]{3,2,1,0:T(8,128)}, u32[]{:S(2)}, u32[]{:S(2)}) collective-permute-start(f32[4,1,16,514]{3,2,1,0:T(8,128)} %get-tuple-element.35), channel_id=1, source_target_pairs={{1,0},{2,1},{3,2},{4,3},{5,4},{6,5},{7,6},{8,7},{9,8},{10,9},{11,1... | collective-permute-start | bytes 394760 | tf_op jit(solution)/shard_map/ppermute | solution.py:29
where the time goes:
time: 356 us; the launch traced here: 352 us
  local copies, waits for them, and re-layouts  273 us (77%)
  starting transfers between devices  50.2 us (14%)
  other arithmetic  13.7 us (4%)
  waiting for transfers between devices  10.6 us (3%)
    gather x2, local copies, waits for them, and re-layouts, body(): jnp.take(level_table, crystal_label_map, axis=1) * frozen_share_map[None]  237 us
    ppermute x5, starting transfers between devices, passed_along(): lax.ppermute(array, axis, [(i, (i + by) % count) for i in range(count)])  33.3 us
    gather x9, local copies, waits for them, and re-layouts, element_matrix(): columns[within, local][None, :]  11.8 us
    ppermute x5, waiting for transfers between devices, passed_along(): lax.ppermute(array, axis, [(i, (i + by) % count) for i in range(count)])  7.88 us
    ppermute x2, starting transfers between devices, extended_2(): after = lax.ppermute(first, axis, down)  7.23 us
  transfers between devices with their start and end apart: 10, of which 4 were waited for; matrix products, arithmetic and copies ran while one was open for 81% of the time, Pallas kernels for 0%

commit v1 on v0

v1 whole, which is shorter than its diff:
```python
import functools

import jax
import jax.numpy as jnp
import numpy as np
from jax import lax
from jax.experimental import pallas as pl
from jax.experimental.pallas import tpu as pltpu
from jax.sharding import PartitionSpec as P

MESH = pl.DeviceIdType.MESH
HIGHEST = lax.Precision.HIGHEST
STEP = 0.004
CHUNK = 64
ROWS = 72


def interpolation_matrix():
    points = (np.arange(8) + 0.5) / 8
    basis = np.stack(
        [
            2.0 * (points - 0.5) * (points - 1.0),
            -4.0 * points * (points - 1.0),
            2.0 * points * (points - 0.5),
        ],
        1,
    )
    along_z = np.zeros((4, 16))
    for c in range(2):
        for p in range(8):
            for k in range(3):
                along_z[(2 * c + k) % 4, 8 * c + p] += basis[p, k]
    plane = np.einsum("nj,zc->jznc", basis, along_z).reshape(12, 128)
    matrix = np.zeros((128, 256), np.float32)
    matrix[16:28, :128] = plane
    matrix[80:92, 128:] = plane
    return matrix


def take_lanes(values, index):
    return jnp.take_along_axis(values, index, axis=1, mode="promise_in_bounds")


def stiffness_action(kappa, shifts):
    odd_x, odd_y, odd_z = shifts.odd

    def spread(values, axis):
        before = shifts.moved(values, axis, -1)
        return jnp.where(
            shifts.odd[axis], (2.0 / 3.0) * values, (1.0 / 6.0) * (values + before)
        )

    def spread_x(values):
        return jnp.where(
            odd_x,
            (2.0 / 3.0) * values,
            (1.0 / 6.0) * (values + shifts.slab(values, -1)),
        )

    over_x = spread_x(kappa)
    fields = (
        spread(spread(kappa, 1), 2) * (1.0 / 3.0),
        spread(over_x, 2) * (1.0 / 3.0),
        spread(over_x, 1) * (1.0 / 3.0),
    )
    centre = None
    pairs = []
    for axis in range(3):
        here = fields[axis]
        if axis == 0:
            before = shifts.slab(here, -1)
        else:
            before = shifts.moved(here, axis, -1)
        part = jnp.where(shifts.odd[axis], 16.0 * here, 7.0 * (here + before))
        centre = part if centre is None else centre + part
        pairs.append((here, jnp.where(shifts.odd[axis], here, before)))

    def act(values):
        total = centre * values
        for axis in range(3):
            ahead, behind = pairs[axis]
            one, two, back, back_two = shifts.neighbours(values, axis)
            odd = shifts.odd[axis]
            total = total + ahead * (jnp.where(odd, 0.0, two) - 8.0 * one)
            total = total + behind * (jnp.where(odd, 0.0, back_two) - 8.0 * back)
        return total

    return act


class Shifts:
    lane_axis = 1

    def lane_roll(self, values, by):
        return pltpu.roll(values, by % 128, self.lane_axis)

    def z_moved(self, values, by):
        z = self.z
        if by == 1:
            return jnp.where(z == 3, self.lane_roll(values, 3), self.lane_roll(values, -1))
        if by == -1:
            return jnp.where(z == 0, self.lane_roll(values, -3), self.lane_roll(values, 1))
        return jnp.where(z >= 2, self.lane_roll(values, 2), self.lane_roll(values, -2))

    def moved(self, values, axis, by):
        if axis == 1:
            return self.y_moved(values, by)
        return self.z_moved(values, by)

    def neighbours(self, values, axis):
        if axis == 0:
            other = self.other(values)
            ahead = jnp.where(self.odd[0], self.slab(other, 1), other)
            behind = jnp.where(self.odd[0], other, self.slab(other, -1))
            return ahead, self.slab(values, 1), behind, self.slab(values, -1)
        if axis == 1:
            return tuple(self.y_moved(values, by) for by in (1, 2, -1, -2))
        two = self.z_moved(values, 2)
        return self.z_moved(values, 1), two, self.z_moved(values, -1), two


class BrickShifts(Shifts):
    def __init__(self, shape):
        lane = lax.broadcasted_iota(jnp.int32, shape, 1)
        self.rows = shape[0]
        self.z = lane & 3
        self.odd = (lane >= 64, (lane & 4) != 0, (lane & 1) != 0)

    def y_moved(self, values, by):
        return self.lane_roll(values, -4 * by)

    def slab(self, values, by):
        return pltpu.roll(values, (-by) % self.rows, 0)

    def other(self, values):
        return self.lane_roll(values, 64)


class SlabShifts(Shifts):
    lane_axis = 2

    def __init__(self, shape):
        self.lane = lax.broadcasted_iota(jnp.int32, shape, 2)
        self.plane = lax.broadcasted_iota(jnp.int32, shape, 1) & 1
        self.z = self.lane & 3
        self.odd = (self.plane != 0, (self.lane & 4) != 0, (self.lane & 1) != 0)

    def y_moved(self, values, by):
        rolled = self.lane_roll(values, -4 * by)
        if by > 0:
            return jnp.where(
                self.lane < 128 - 4 * by, rolled, pltpu.roll(rolled, 6, 1)
            )
        return jnp.where(self.lane >= -4 * by, rolled, pltpu.roll(rolled, 2, 1))

    def slab(self, values, by):
        if by == 1:
            return jnp.concatenate([values[1:], values[:1]], 0)
        return jnp.concatenate([values[-1:], values[:-1]], 0)

    def other(self, values):
        return jnp.where(self.plane == 0, pltpu.roll(values, 7, 1), pltpu.roll(values, 1, 1))


def inverse_mass(shifts):
    odd_x, odd_y, odd_z = shifts.odd
    return (
        jnp.where(odd_x, 1.5, 3.0) * jnp.where(odd_y, 1.5, 3.0) * jnp.where(odd_z, 1.5, 3.0)
    )


def heat_step(field, heat, kappa, shifts):
    act = stiffness_action(kappa, shifts)
    inverse = inverse_mass(shifts)
    rate_one = (heat - act(field)) * inverse
    middle = field + STEP * rate_one
    rate_two = (heat - act(middle)) * inverse
    return field + (0.5 * STEP) * (rate_one + rate_two)


def blocks(values):
    return jnp.concatenate([values[:, 128 * q : 128 * q + 128] for q in range(4)], 0)


def lookup(table_ref, labels):
    low = labels & 127
    high = labels >> 8
    found = jnp.zeros(labels.shape, jnp.int32)
    for row in range(32):
        words = jnp.broadcast_to(table_ref[row : row + 1, :], labels.shape)
        found = jnp.where(high == row, take_lanes(words, low), found)
    return jnp.where((labels & 128) != 0, found >> 12, found & 4095)


def kernel(
    groups,
    slabs,
    field_ref,
    kappa_ref,
    heat_ref,
    solid_ref,
    label_ref,
    table_ref,
    slot_ref,
    seed_ref,
    matrix_ref,
    new_field_ref,
    new_solid_ref,
    outbox,
    inbox,
    near_field,
    near_heat,
    near_kappa,
    words,
    ahead_x,
    behind_x,
    ahead_y,
    behind_y,
    from_ahead_x,
    from_behind_x,
    from_ahead_y,
    from_behind_y,
    gathered,
    nucleation,
    planes,
    tally,
    box_sems,
    near_sems,
    near_send_sems,
    edge_recv_sems,
    edge_send_sems,
):
    g = lax.axis_index("grp")
    h = lax.axis_index("slab")
    g_next = lax.rem(g + 1, groups)
    g_prev = lax.rem(g + groups - 1, groups)
    high_edge = h >= slabs - 2
    low_edge = h <= 2

    barrier = pltpu.get_barrier_semaphore()

    def greet(to_g, to_h):
        pl.semaphore_signal(barrier, inc=1, device_id=(to_g, to_h), device_id_type=MESH)

    greet(g_prev, jnp.int32(slabs - 2))
    greet(g_prev, jnp.int32(slabs - 1))
    for first in range(3):
        greet(g_next, jnp.int32(first))
    greet(g_prev, h)
    greet(g_next, h)

    def greet_group(step, carry):
        greet(g, lax.rem(h + 1 + step, slabs))
        return carry

    lax.fori_loop(0, slabs - 1, greet_group, 0)

    sub = lax.broadcasted_iota(jnp.int32, (8, 128), 0)
    lane = lax.broadcasted_iota(jnp.int32, (8, 128), 1)
    window = 8 * sub + (lane & 63)
    even_lane = lane < 64
    kappa_lane = (lane >= 44) & (lane < 56)
    kappa_rows = jnp.broadcast_to(kappa_ref[...], (8, 128))
    shifted_field = [pltpu.roll(field_ref[...], 16, 1), pltpu.roll(field_ref[...], 512 - 48, 1)]
    shifted_heat = [pltpu.roll(heat_ref[...], 16, 1), pltpu.roll(heat_ref[...], 512 - 48, 1)]

    def windows(shifted, m):
        part = shifted[m % 2][:, 128 * (m // 2) : 128 * (m // 2) + 128]
        even = take_lanes(jnp.broadcast_to(part[0:1], (8, 128)), window)
        odd = take_lanes(jnp.broadcast_to(part[1:2], (8, 128)), window)
        return jnp.where(even_lane, even, odd)

    for m in range(slabs // 8):
        outbox[8 * m : 8 * m + 8, 0:128] = windows(shifted_field, m)
        index = (2 * (8 * m + sub) - 4 + lane - 44) & 127
        outbox[8 * m : 8 * m + 8, 128:256] = jnp.where(
            kappa_lane, take_lanes(kappa_rows, index), windows(shifted_heat, m)
        )

    expected = 63 + 2 + jnp.where(high_edge, slabs, 0) + jnp.where(low_edge, slabs, 0)
    pl.semaphore_wait(barrier, expected)

    def post(to_g, to_h, row):
        return pltpu.make_async_remote_copy(
            src_ref=outbox.at[pl.ds(to_h, 1), :],
            dst_ref=inbox.at[pl.ds(row, 1), :],
            send_sem=box_sems.at[0],
            recv_sem=box_sems.at[1],
            device_id=(to_g, to_h),
            device_id_type=MESH,
        )

    def wait_messages(many, kind):
        size = tally.at[pl.ds(0, many)]
        pltpu.make_async_copy(size, size, box_sems.at[kind]).wait()

    here = g * slabs + h
    count = groups * slabs
    near = []
    for by in (1, -1, 2, -2):
        there = lax.rem(here + by + count, count)
        device = (there // slabs, lax.rem(there, slabs))
        slot = {2: 0, 1: 1, -1: 2, -2: 3}[by]
        pairs = [(field_ref, near_field, slot, 0)]
        if by in (1, -1):
            pairs.append((heat_ref, near_heat, slot - 1, 1))
        if by != -2:
            pairs.append((kappa_ref, near_kappa, slot, 2))
        for source, target, place, kind in pairs:
            copy = pltpu.make_async_remote_copy(
                src_ref=source,
                dst_ref=target.at[place],
                send_sem=near_send_sems.at[slot, kind],
                recv_sem=near_sems.at[slot, kind],
                device_id=device,
                device_id_type=MESH,
            )
            copy.start()
            near.append(copy)

    def post_group(step, carry):
        to_h = lax.rem(h + 1 + step, slabs)
        post(g, to_h, h + 2).start()
        return carry

    @pl.when(high_edge)
    def _():
        def body(to_h, carry):
            post(g_next, to_h, h - (slabs - 2)).start()
            return carry

        lax.fori_loop(0, slabs, body, 0)

    @pl.when(low_edge)
    def _():
        def body(to_h, carry):
            post(g_prev, to_h, h + slabs + 2).start()
            return carry

        lax.fori_loop(0, slabs, body, 0)

    lax.fori_loop(0, slabs - 1, post_group, 0)

    weight = 1 << (2 * lax.broadcasted_iota(jnp.int32, (6, 1), 0))
    codes = jnp.sum((table_ref[...] - 1) * weight, axis=0, keepdims=True)
    words[...] = jnp.zeros(words.shape, jnp.int32)
    for row in range(31):
        low_half = codes[:, 256 * row : 256 * row + 128]
        high_half = codes[:, 256 * row + 128 : 256 * row + 256]
        words[row : row + 1, :] = low_half | (high_half << 12)
    words[31:32, 0:64] = codes[:, 7936:8000]

    lane_c = lax.broadcasted_iota(jnp.int32, (CHUNK, 128), 1)
    depth = lane_c & 15

    def cells(c, carry):
        rows = pl.ds(pl.multiple_of(c * CHUNK, CHUNK), CHUNK)
        code = lookup(words, label_ref[rows, :])
        quarter = 0.25 * solid_ref[rows, :]

        def weighted(d):
            return quarter * (((code >> (2 * d)) & 3) + 1).astype(jnp.float32)

        ahead_x[rows, :] = weighted(0)
        behind_x[rows, :] = weighted(1)
        up_y = weighted(2)
        down_y = weighted(3)
        up_z = weighted(4)
        down_z = weighted(5)
        gathered[rows, :] = (
            jnp.where(depth == 15, pltpu.roll(up_z, 15, 1), pltpu.roll(up_z, 127, 1))
            + jnp.where(depth == 0, pltpu.roll(down_z, 113, 1), pltpu.roll(down_z, 1, 1))
            + jnp.where(lane_c < 112, pltpu.roll(up_y, 112, 1), 0.0)
            + jnp.where(lane_c >= 16, pltpu.roll(down_y, 16, 1), 0.0)
        )
        mine = (lane_c >> 4) == c
        ahead_y[...] = jnp.where(mine, pltpu.roll(up_y, 16 * c, 1), ahead_y[...])
        behind_y[...] = jnp.where(
            mine, pltpu.roll(down_y, lax.rem(16 * c + 16, 128), 1), behind_y[...]
        )
        return carry

    ahead_y[...] = jnp.zeros(ahead_y.shape, jnp.float32)
    behind_y[...] = jnp.zeros(behind_y.shape, jnp.float32)
    edge_x = solid_ref.shape[0]
    lax.fori_loop(0, edge_x // CHUNK, cells, 0)

    total = jnp.zeros((edge_x, 128), jnp.float32)
    cell_row = lax.broadcasted_iota(jnp.int32, (edge_x, 128), 0)
    cell_lane = lax.broadcasted_iota(jnp.int32, (128, 128), 0)
    for part in range(2):
        slots = slot_ref[part : part + 1, :]
        code = lookup(words, jnp.broadcast_to(seed_ref[part : part + 1, :], (8, 128)))
        level = jnp.full((8, 128), 6, jnp.int32)
        for d in range(6):
            level = level + ((code >> (2 * d)) & 3)
        level = level[0:1].astype(jnp.float32)
        at_row = jnp.where(cell_row == (slots >> 7), 1.0, 0.0).astype(jnp.bfloat16)
        at_lane = jnp.where(cell_lane == (slots & 127), level, 0.0).astype(jnp.bfloat16)
        total = total + lax.dot_general(
            at_row, at_lane, (((1,), (1,)), ((), ())), preferred_element_type=jnp.float32
        )
    nucleation[...] = total * (1.0 / 6.0)

    h_next = lax.rem(h + 1, slabs)
    h_prev = lax.rem(h + slabs - 1, slabs)
    edges = []
    for number, (source, target, device) in enumerate(
        (
            (ahead_y, from_ahead_y, (g, h_prev)),
            (behind_y, from_behind_y, (g, h_next)),
            (ahead_x.at[0:8, :], from_ahead_x, (g_prev, h)),
            (behind_x.at[edge_x - 8 : edge_x, :], from_behind_x, (g_next, h)),
        )
    ):
        copy = pltpu.make_async_remote_copy(
            src_ref=source,
            dst_ref=target,
            send_sem=edge_send_sems.at[number],
            recv_sem=edge_recv_sems.at[number],
            device_id=device,
            device_id_type=MESH,
        )
        copy.start()
        edges.append(copy)

    gathered[0 : edge_x - 1, :] = gathered[0 : edge_x - 1, :] + ahead_x[1:edge_x, :]
    gathered[1:edge_x, :] = gathered[1:edge_x, :] + behind_x[0 : edge_x - 1, :]

    for copy in near:
        copy.wait_recv()
    zero = jnp.zeros((8, 128), jnp.float32)
    stacked_field = jnp.stack(
        [
            blocks(near_field[0]),
            blocks(near_field[1]),
            blocks(field_ref[...]),
            blocks(near_field[2]),
            blocks(near_field[3]),
        ],
        0,
    )
    stacked_heat = jnp.stack(
        [zero, blocks(near_heat[0]), blocks(heat_ref[...]), blocks(near_heat[1]), zero], 0
    )

    block_of = sub >> 1

    def expanded(row):
        index = block_of * 32 + (lane >> 3) * 2 + ((lane >> 1) & 1)
        return take_lanes(jnp.broadcast_to(row, (8, 128)), index)

    stacked_kappa = jnp.stack(
        [
            expanded(near_kappa[0]),
            expanded(near_kappa[1]),
            expanded(kappa_ref[...]),
            expanded(near_kappa[2]),
            zero,
        ],
        0,
    )
    moved = heat_step(
        stacked_field, stacked_heat, stacked_kappa, SlabShifts((5, 8, 128))
    )[2]
    for q in range(4):
        new_field_ref[:, 128 * q : 128 * q + 128] = moved[2 * q : 2 * q + 2, :]

    inbox[pl.ds(h + 2, 1), :] = outbox[pl.ds(h, 1), :]
    wait_messages(slabs + 4, 1)
    shifts = BrickShifts((ROWS, 128))
    box_lane = lax.broadcasted_iota(jnp.int32, (ROWS, 128), 1)
    half = box_lane & 63
    brick_heat = inbox[:, 128:256]
    brick_kappa = take_lanes(
        brick_heat, jnp.minimum(44 + (half >> 3) * 2 + ((half >> 1) & 1), 55)
    )
    brick = heat_step(inbox[:, 0:128], brick_heat, brick_kappa, shifts)
    box_row = lax.broadcasted_iota(jnp.int32, (ROWS, 128), 0)
    wanted = (half >= 16) & (half < 28) & (box_row >= 2) & (box_row < slabs + 3)
    brick = pltpu.roll(jnp.where(wanted, brick, 0.0), ROWS - 2, 0)
    pair = jnp.dot(
        brick, matrix_ref[...], precision=HIGHEST, preferred_element_type=jnp.float32
    )
    planes[:, 0:256] = pair
    planes[:, 256:384] = pltpu.roll(pair[:, 0:128], ROWS - 1, 0)

    for copy in edges:
        copy.wait_recv()
    gathered[edge_x - 1 : edge_x, :] = gathered[edge_x - 1 : edge_x, :] + from_ahead_x[0:1, :]
    gathered[0:1, :] = gathered[0:1, :] + from_behind_x[7:8, :]
    point = (sub.astype(jnp.float32) + 0.5) * 0.125
    basis = (
        2.0 * (point - 0.5) * (point - 1.0),
        -4.0 * point * (point - 1.0),
        2.0 * point * (point - 0.5),
    )

    def finish(c, carry):
        rows = pl.ds(pl.multiple_of(c * CHUNK, CHUNK), CHUNK)
        layer = planes[pl.ds(pl.multiple_of(c * (CHUNK // 8), CHUNK // 8), CHUNK // 8), :]
        parts = []
        for k in range(CHUNK // 8):
            parts.append(
                basis[0] * layer[k : k + 1, 0:128]
                + basis[1] * layer[k : k + 1, 128:256]
                + basis[2] * layer[k : k + 1, 256:384]
            )
        under = jnp.maximum(-jnp.concatenate(parts, 0), 0.0)
        side = jnp.where(
            lane_c >= 112,
            pltpu.roll(from_ahead_y[...], lax.rem(240 - 16 * c, 128), 1),
            jnp.where(
                lane_c < 16, pltpu.roll(from_behind_y[...], lax.rem(128 - 16 * c, 128), 1), 0.0
            ),
        )
        rate = under * (under * (gathered[rows, :] + side) + nucleation[rows, :])
        solid = solid_ref[rows, :]
        new_solid_ref[rows, :] = solid + (1.0 - solid) * (1.0 - jnp.exp(-rate))
        return carry

    lax.fori_loop(0, edge_x // CHUNK, finish, 0)

    for copy in near + edges:
        copy.wait_send()
    @pl.when(high_edge | low_edge)
    def _():
        wait_messages(2 * slabs - 1, 0)

    @pl.when(jnp.logical_not(high_edge | low_edge))
    def _():
        wait_messages(slabs - 1, 0)


def solution(mesh):
    groups, slabs = mesh.shape["grp"], mesh.shape["slab"]
    matrix = interpolation_matrix()

    def body(field, kappa, heat, solid, label, table, slot, seed):
        vmem = pl.BlockSpec(memory_space=pltpu.VMEM)
        edge_x = solid.shape[0]
        f32 = jnp.float32
        return pl.pallas_call(
            functools.partial(kernel, groups, slabs),
            out_shape=(
                jax.ShapeDtypeStruct(field.shape, f32),
                jax.ShapeDtypeStruct(solid.shape, f32),
            ),
            in_specs=[vmem] * 9,
            out_specs=(vmem, vmem),
            scratch_shapes=[
                pltpu.VMEM((slabs, 256), f32),
                pltpu.VMEM((ROWS, 256), f32),
                pltpu.VMEM((4, 2, 512), f32),
                pltpu.VMEM((2, 2, 512), f32),
                pltpu.VMEM((3, 1, 128), f32),
                pltpu.VMEM((32, 128), jnp.int32),
                pltpu.VMEM((edge_x, 128), f32),
                pltpu.VMEM((edge_x, 128), f32),
                pltpu.VMEM((CHUNK, 128), f32),
                pltpu.VMEM((CHUNK, 128), f32),
                pltpu.VMEM((8, 128), f32),
                pltpu.VMEM((8, 128), f32),
                pltpu.VMEM((CHUNK, 128), f32),
                pltpu.VMEM((CHUNK, 128), f32),
                pltpu.VMEM((edge_x, 128), f32),
                pltpu.VMEM((edge_x, 128), f32),
                pltpu.VMEM((ROWS, 384), f32),
                pltpu.VMEM((2 * slabs, 2, 128), f32),
                pltpu.SemaphoreType.DMA((2,)),
                pltpu.SemaphoreType.DMA((4, 3)),
                pltpu.SemaphoreType.DMA((4, 3)),
                pltpu.SemaphoreType.DMA((4,)),
                pltpu.SemaphoreType.DMA((4,)),
            ],
            compiler_params=pltpu.CompilerParams(collective_id=0, has_side_effects=True),
        )(
            field,
            kappa,
            heat,
            solid,
            label,
            table.T,
            slot.reshape(2, 128),
            seed.reshape(2, 128),
            jnp.asarray(matrix),
        )

    in_specs = (
        P(("grp", "slab"), None),
        P(("grp", "slab"), None),
        P(("grp", "slab"), None),
        P("grp", "slab"),
        P("grp", "slab"),
        P(),
        P(("grp", "slab")),
        P(("grp", "slab")),
    )
    out_specs = (P(("grp", "slab"), None), P("grp", "slab"))
    return jax.shard_map(body, mesh=mesh, in_specs=in_specs, out_specs=out_specs, check_vma=False)
```

time: 356 us -> 37.6 us (0.11); the launches traced: 352 us -> 37.4 us
  local copies, waits for them, and re-layouts: 273 us -> 2.95 us
  starting transfers between devices: 50.2 us -> 0 us
  Pallas kernels: 0 us -> 33.8 us
  other arithmetic: 13.7 us -> 0 us
  waiting for transfers between devices: 10.6 us -> 0 us
    gather x12 -> x0, local copies, waits for them, and re-layouts: 251 us -> none  [the longest x2 237 us: body(): jnp.take(level_table, crystal_label_map, axis=1) * frozen_share_map[None]]
    ppermute x9 -> x0, starting transfers between devices: 45.9 us -> none  [the longest x5 33.3 us: passed_along(): lax.ppermute(array, axis, [(i, (i + by) % count) for i in range(count)])]
    pallas_call x0 -> x1, Pallas kernels: none -> 33.8 us  [body(): pl.pallas_call(functools.partial(kernel, groups, slabs), out_shape=(jax.S...]
    ppermute x9 -> x0, waiting for transfers between devices: 10.6 us -> none  [the longest x5 7.88 us: passed_along(): lax.ppermute(array, axis, [(i, (i + by) % count) for i in range(count)])]
    slice x26 -> x0, local copies, waits for them, and re-layouts: 5.75 us -> none  [the longest x2 2.62 us: body(): weighted[:4].reshape(4, edge_x, edge_y, depth)]
    mul x27 -> x0, local copies, waits for them, and re-layouts: 5.43 us -> none  [the longest x12 3.63 us: contract(): terms.append(WEIGHTS[point] * coefficient * slope)]
    add x20 -> x0, other arithmetic: 4.68 us -> none  [the longest x1 2.01 us: body(): frozen_share_map + (1.0 - frozen_share_map) * (1.0 - jnp.exp(-capture_rate))]
    all_to_all x1 -> x0, starting transfers between devices: 4.36 us -> none  [body(): lax.all_to_all(slab_cells, 'slab', split_axis=1, concat_axis=0, tiled=True)]
  transfers between devices with their start and end apart: 10 -> 0, of which waited for: 4 -> 0; matrix products, arithmetic and copies ran while one was open for 81% -> 0% of each run, Pallas kernels for 0% -> 0%
where the time goes in v1:
time: 37.6 us; the launch traced here: 37.4 us
  Pallas kernels  33.8 us (90%)
  local copies, waits for them, and re-layouts  2.95 us (8%)
  between operations  0.64 us (2%)
    pallas_call x1, Pallas kernels, body(): pl.pallas_call(functools.partial(kernel, groups, slabs), out_shape=(jax.S...  33.8 us
    unnamed x2, local copies, waits for them, and re-layouts  2.95 us

profile of v1, /device:TPU:1, one launch (start us, length us, event | category | flops | bytes accessed | tf_op | source)
XLA Modules:
  0.0 37.4 jit_solution(10760918084997697224)
XLA Ops:
  0.6 33.8 %shard_map.104 = (f32[2,512]{1,0:T(2,128)}, f32[512,128]{1,0:T(8,128)}) custom-call(f32[2,512]{1,0:T(2,128)} %field_ref.1, f32[1,128]{1,0:T(1,128)} %kappa_ref.1, f32[2,512]{1,0:T(2,128)} %heat_ref.1, f32[512,128]{1,0:T(8,128)} %solid_ref.1, s32[512,128]{1,0:T(8,128)} %label_ref.1, s32[6,8000]{1,0:T(8,128)} %bitcast.3, s32[2,128]{1,0:T(2,128)} %bitcast.4, ...), custom_call_target="tpu_custom_call" | custom-call | tf_op jit(solution)/shard_map/pallas_call | solution.py:543
  34.5 1.3 %copy.13 = f32[2,512]{1,0:T(2,128)} copy(f32[2,512]{1,0:T(2,128)} %get-tuple-element.4) | data formatting | bytes 8192
  35.8 1.7 %copy.14 = f32[512,128]{1,0:T(8,128)} copy(f32[512,128]{1,0:T(8,128)} %get-tuple-element.5) | data formatting | bytes 524288

commit v2 on v1

--- a/solution.py
+++ b/solution.py
@@ -184,28 +184,46 @@
 
 def lookup(table_ref, labels):
     low = labels & 127
-    high = labels >> 8
-    found = jnp.zeros(labels.shape, jnp.int32)
-    for row in range(32):
-        words = jnp.broadcast_to(table_ref[row : row + 1, :], labels.shape)
-        found = jnp.where(high == row, take_lanes(words, low), found)
+    bits = [(labels & (256 << level)) != 0 for level in range(5)]
+
+    def choose(first, level):
+        if level < 0:
+            return take_lanes(table_ref[8 * first : 8 * first + 8, :], low)
+        return jnp.where(
+            bits[level], choose(first + (1 << level), level - 1), choose(first, level - 1)
+        )
+
+    found = choose(0, 4)
     return jnp.where((labels & 128) != 0, found >> 12, found & 4095)
 
 
-def kernel(
+def exchange(
     groups,
     slabs,
+    field_any,
+    kappa_any,
+    heat_any,
+    solid_any,
+    label_any,
+    table_any,
+    slot_any,
+    seed_any,
+    matrix_any,
+    new_field_ref,
+    solid_ref,
+    planes,
+    gathered,
+    nucleation,
+    side_ahead,
+    side_behind,
     field_ref,
     kappa_ref,
     heat_ref,
-    solid_ref,
     label_ref,
     table_ref,
     slot_ref,
     seed_ref,
     matrix_ref,
-    new_field_ref,
-    new_solid_ref,
     outbox,
     inbox,
     near_field,
@@ -220,16 +238,31 @@
     from_behind_x,
     from_ahead_y,
     from_behind_y,
-    gathered,
-    nucleation,
-    planes,
     tally,
+    load_sems,
     box_sems,
     near_sems,
     near_send_sems,
     edge_recv_sems,
     edge_send_sems,
 ):
+    loads = []
+    for number, (source, target) in enumerate(
+        (
+            (field_any, field_ref),
+            (heat_any, heat_ref),
+            (kappa_any, kappa_ref),
+            (table_any, table_ref),
+            (label_any, label_ref),
+            (solid_any, solid_ref),
+            (slot_any, slot_ref),
+            (seed_any, seed_ref),
+            (matrix_any, matrix_ref),
+        )
+    ):
+        copy = pltpu.make_async_copy(source, target, load_sems.at[number])
+        copy.start()
+        loads.append(copy)
     g = lax.axis_index("grp")
     h = lax.axis_index("slab")
     g_next = lax.rem(g + 1, groups)
@@ -255,6 +288,8 @@
 
     lax.fori_loop(0, slabs - 1, greet_group, 0)
 
+    for copy in loads[:3]:
+        copy.wait()
     sub = lax.broadcasted_iota(jnp.int32, (8, 128), 0)
     lane = lax.broadcasted_iota(jnp.int32, (8, 128), 1)
     window = 8 * sub + (lane & 63)
@@ -276,6 +311,61 @@
         outbox[8 * m : 8 * m + 8, 128:256] = jnp.where(
             kappa_lane, take_lanes(kappa_rows, index), windows(shifted_heat, m)
         )
+
+    for copy in loads[3:]:
+        copy.wait()
+    weight = 1 << (2 * lax.broadcasted_iota(jnp.int32, (6, 1), 0))
+    codes = jnp.sum((table_ref[...] - 1) * weight, axis=0, keepdims=True)
+    for row in range(31):
+        low_half = codes[:, 256 * row : 256 * row + 128]
+        high_half = codes[:, 256 * row + 128 : 256 * row + 256]
+        words[8 * row : 8 * row + 8, :] = jnp.broadcast_to(
+            low_half | (high_half << 12), (8, 128)
+        )
+    rest = jnp.concatenate([codes[:, 7936:8000], jnp.zeros((1, 64), jnp.int32)], 1)
+    words[248:256, :] = jnp.broadcast_to(rest, (8, 128))
+
+    lane_c = lax.broadcasted_iota(jnp.int32, (CHUNK, 128), 1)
+    depth = lane_c & 15
+
+    def cells(c, carry):
+        rows = pl.ds(pl.multiple_of(c * CHUNK, CHUNK), CHUNK)
+        labels = label_ref[rows, :]
+        code = jnp.concatenate(
+            [lookup(words, labels[8 * k : 8 * k + 8]) for k in range(CHUNK // 8)], 0
+        )
+        quarter = 0.25 * solid_ref[rows, :]
+
+        def weighted(d):
+            return quarter * (((code >> (2 * d)) & 3) + 1).astype(jnp.float32)
+
+        ahead_x[rows, :] = weighted(0)
+        behind_x[rows, :] = weighted(1)
+        up_y = weighted(2)
+        down_y = weighted(3)
+        up_z = weighted(4)
+        down_z = weighted(5)
+        gathered[rows, :] = (
+            jnp.where(depth == 15, pltpu.roll(up_z, 15, 1), pltpu.roll(up_z, 127, 1))
+            + jnp.where(depth == 0, pltpu.roll(down_z, 113, 1), pltpu.roll(down_z, 1, 1))
+            + jnp.where(lane_c < 112, pltpu.roll(up_y, 112, 1), 0.0)
+            + jnp.where(lane_c >= 16, pltpu.roll(down_y, 16, 1), 0.0)
+        )
+        mine = (lane_c >> 4) == c
+        ahead_y[...] = jnp.where(mine, pltpu.roll(up_y, 16 * c, 1), ahead_y[...])
+        behind_y[...] = jnp.where(
+            mine, pltpu.roll(down_y, lax.rem(16 * c + 16, 128), 1), behind_y[...]
+        )
+        return carry
+
+    ahead_y[...] = jnp.zeros(ahead_y.shape, jnp.float32)
+    behind_y[...] = jnp.zeros(behind_y.shape, jnp.float32)
+    edge_x = solid_ref.shape[0]
+    chunks = edge_x // CHUNK
+    x, y = lax.rem(h // 2, 4), h // 8
+    hops = jnp.abs(x - 2) + jnp.abs(y - 4)
+    ahead = jnp.where(g == 0, chunks, jnp.minimum(2 * hops, chunks))
+    lax.fori_loop(0, ahead, cells, 0)
 
     expected = 63 + 2 + jnp.where(high_edge, slabs, 0) + jnp.where(low_edge, slabs, 0)
     pl.semaphore_wait(barrier, expected)
@@ -341,49 +431,7 @@
 
     lax.fori_loop(0, slabs - 1, post_group, 0)
 
-    weight = 1 << (2 * lax.broadcasted_iota(jnp.int32, (6, 1), 0))
-    codes = jnp.sum((table_ref[...] - 1) * weight, axis=0, keepdims=True)
-    words[...] = jnp.zeros(words.shape, jnp.int32)
-    for row in range(31):
-        low_half = codes[:, 256 * row : 256 * row + 128]
-        high_half = codes[:, 256 * row + 128 : 256 * row + 256]
-        words[row : row + 1, :] = low_half | (high_half << 12)
-    words[31:32, 0:64] = codes[:, 7936:8000]
-
-    lane_c = lax.broadcasted_iota(jnp.int32, (CHUNK, 128), 1)
-    depth = lane_c & 15
-
-    def cells(c, carry):
-        rows = pl.ds(pl.multiple_of(c * CHUNK, CHUNK), CHUNK)
-        code = lookup(words, label_ref[rows, :])
-        quarter = 0.25 * solid_ref[rows, :]
-
-        def weighted(d):
-            return quarter * (((code >> (2 * d)) & 3) + 1).astype(jnp.float32)
-
-        ahead_x[rows, :] = weighted(0)
-        behind_x[rows, :] = weighted(1)
-        up_y = weighted(2)
-        down_y = weighted(3)
-        up_z = weighted(4)
-        down_z = weighted(5)
-        gathered[rows, :] = (
-            jnp.where(depth == 15, pltpu.roll(up_z, 15, 1), pltpu.roll(up_z, 127, 1))
-            + jnp.where(depth == 0, pltpu.roll(down_z, 113, 1), pltpu.roll(down_z, 1, 1))
-            + jnp.where(lane_c < 112, pltpu.roll(up_y, 112, 1), 0.0)
-            + jnp.where(lane_c >= 16, pltpu.roll(down_y, 16, 1), 0.0)
-        )
-        mine = (lane_c >> 4) == c
-        ahead_y[...] = jnp.where(mine, pltpu.roll(up_y, 16 * c, 1), ahead_y[...])
-        behind_y[...] = jnp.where(
-            mine, pltpu.roll(down_y, lax.rem(16 * c + 16, 128), 1), behind_y[...]
-        )
-        return carry
-
-    ahead_y[...] = jnp.zeros(ahead_y.shape, jnp.float32)
-    behind_y[...] = jnp.zeros(behind_y.shape, jnp.float32)
-    edge_x = solid_ref.shape[0]
-    lax.fori_loop(0, edge_x // CHUNK, cells, 0)
+    lax.fori_loop(ahead, chunks, cells, 0)
 
     total = jnp.zeros((edge_x, 128), jnp.float32)
     cell_row = lax.broadcasted_iota(jnp.int32, (edge_x, 128), 0)
@@ -489,16 +537,48 @@
         copy.wait_recv()
     gathered[edge_x - 1 : edge_x, :] = gathered[edge_x - 1 : edge_x, :] + from_ahead_x[0:1, :]
     gathered[0:1, :] = gathered[0:1, :] + from_behind_x[7:8, :]
+    side_ahead[...] = from_ahead_y[...]
+    side_behind[...] = from_behind_y[...]
+
+    for copy in near + edges:
+        copy.wait_send()
+    @pl.when(high_edge | low_edge)
+    def _():
+        wait_messages(2 * slabs - 1, 0)
+
+    @pl.when(jnp.logical_not(high_edge | low_edge))
+    def _():
+        wait_messages(slabs - 1, 0)
+
+
+def finish(
+    field_ref,
+    solid_ref,
+    planes,
+    gathered,
+    nucleation,
+    side_ahead,
+    side_behind,
+    new_field_any,
+    new_solid_any,
+    result,
+    sems,
+):
+    chunks = solid_ref.shape[0] // CHUNK
+    field_out = pltpu.make_async_copy(field_ref, new_field_any, sems.at[chunks])
+    field_out.start()
+    sub = lax.broadcasted_iota(jnp.int32, (8, 128), 0)
+    lane_c = lax.broadcasted_iota(jnp.int32, (CHUNK, 128), 1)
     point = (sub.astype(jnp.float32) + 0.5) * 0.125
     basis = (
         2.0 * (point - 0.5) * (point - 1.0),
         -4.0 * point * (point - 1.0),
         2.0 * point * (point - 0.5),
     )
-
-    def finish(c, carry):
-        rows = pl.ds(pl.multiple_of(c * CHUNK, CHUNK), CHUNK)
-        layer = planes[pl.ds(pl.multiple_of(c * (CHUNK // 8), CHUNK // 8), CHUNK // 8), :]
+    stores = []
+    for c in range(chunks):
+        rows = slice(c * CHUNK, (c + 1) * CHUNK)
+        layer = planes[c * (CHUNK // 8) : (c + 1) * (CHUNK // 8), :]
         parts = []
         for k in range(CHUNK // 8):
             parts.append(
@@ -509,27 +589,18 @@
         under = jnp.maximum(-jnp.concatenate(parts, 0), 0.0)
         side = jnp.where(
             lane_c >= 112,
-            pltpu.roll(from_ahead_y[...], lax.rem(240 - 16 * c, 128), 1),
-            jnp.where(
-                lane_c < 16, pltpu.roll(from_behind_y[...], lax.rem(128 - 16 * c, 128), 1), 0.0
-            ),
+            pltpu.roll(side_ahead[...], (240 - 16 * c) % 128, 1),
+            jnp.where(lane_c < 16, pltpu.roll(side_behind[...], (128 - 16 * c) % 128, 1), 0.0),
         )
         rate = under * (under * (gathered[rows, :] + side) + nucleation[rows, :])
         solid = solid_ref[rows, :]
-        new_solid_ref[rows, :] = solid + (1.0 - solid) * (1.0 - jnp.exp(-rate))
-        return carry
-
-    lax.fori_loop(0, edge_x // CHUNK, finish, 0)
-
-    for copy in near + edges:
-        copy.wait_send()
-    @pl.when(high_edge | low_edge)
-    def _():
-        wait_messages(2 * slabs - 1, 0)
-
-    @pl.when(jnp.logical_not(high_edge | low_edge))
-    def _():
-        wait_messages(slabs - 1, 0)
+        result[rows, :] = solid + (1.0 - solid) * (1.0 - jnp.exp(-rate))
+        copy = pltpu.make_async_copy(result.at[rows, :], new_solid_any.at[rows, :], sems.at[c])
+        copy.start()
+        stores.append(copy)
+    for copy in stores:
+        copy.wait()
+    field_out.wait()
 
 
 def solution(mesh):
@@ -538,35 +609,48 @@
 
     def body(field, kappa, heat, solid, label, table, slot, seed):
         vmem = pl.BlockSpec(memory_space=pltpu.VMEM)
+        anywhere = pl.BlockSpec(memory_space=pl.ANY)
         edge_x = solid.shape[0]
-        f32 = jnp.float32
-        return pl.pallas_call(
-            functools.partial(kernel, groups, slabs),
+        f32, i32 = jnp.float32, jnp.int32
+        cells = (edge_x, 128)
+        found = pl.pallas_call(
+            functools.partial(exchange, groups, slabs),
             out_shape=(
                 jax.ShapeDtypeStruct(field.shape, f32),
-                jax.ShapeDtypeStruct(solid.shape, f32),
+                jax.ShapeDtypeStruct(cells, f32),
+                jax.ShapeDtypeStruct((ROWS, 384), f32),
+                jax.ShapeDtypeStruct(cells, f32),
+                jax.ShapeDtypeStruct(cells, f32),
+                jax.ShapeDtypeStruct((CHUNK, 128), f32),
+                jax.ShapeDtypeStruct((CHUNK, 128), f32),
             ),
-            in_specs=[vmem] * 9,
-            out_specs=(vmem, vmem),
+            in_specs=[anywhere] * 9,
+            out_specs=(vmem,) * 7,
             scratch_shapes=[
+                pltpu.VMEM(field.shape, f32),
+                pltpu.VMEM(kappa.shape, f32),
+                pltpu.VMEM(heat.shape, f32),
+                pltpu.VMEM(cells, i32),
+                pltpu.VMEM(table.shape[::-1], i32),
+                pltpu.VMEM((2, 128), i32),
+                pltpu.VMEM((2, 128), i32),
+                pltpu.VMEM(matrix.shape, f32),
                 pltpu.VMEM((slabs, 256), f32),
                 pltpu.VMEM((ROWS, 256), f32),
                 pltpu.VMEM((4, 2, 512), f32),
                 pltpu.VMEM((2, 2, 512), f32),
                 pltpu.VMEM((3, 1, 128), f32),
-                pltpu.VMEM((32, 128), jnp.int32),
-                pltpu.VMEM((edge_x, 128), f32),
-                pltpu.VMEM((edge_x, 128), f32),
+                pltpu.VMEM((256, 128), i32),
+                pltpu.VMEM(cells, f32),
+                pltpu.VMEM(cells, f32),
                 pltpu.VMEM((CHUNK, 128), f32),
                 pltpu.VMEM((CHUNK, 128), f32),
                 pltpu.VMEM((8, 128), f32),
                 pltpu.VMEM((8, 128), f32),
                 pltpu.VMEM((CHUNK, 128), f32),
                 pltpu.VMEM((CHUNK, 128), f32),
-                pltpu.VMEM((edge_x, 128), f32),
-                pltpu.VMEM((edge_x, 128), f32),
-                pltpu.VMEM((ROWS, 384), f32),
                 pltpu.VMEM((2 * slabs, 2, 128), f32),
+                pltpu.SemaphoreType.DMA((9,)),
                 pltpu.SemaphoreType.DMA((2,)),
                 pltpu.SemaphoreType.DMA((4, 3)),
                 pltpu.SemaphoreType.DMA((4, 3)),
@@ -585,6 +669,19 @@
             seed.reshape(2, 128),
             jnp.asarray(matrix),
         )
+        return pl.pallas_call(
+            finish,
+            out_shape=(
+                jax.ShapeDtypeStruct(field.shape, f32),
+                jax.ShapeDtypeStruct(solid.shape, f32),
+            ),
+            in_specs=[vmem] * 7,
+            out_specs=(anywhere, anywhere),
+            scratch_shapes=[
+                pltpu.VMEM(cells, f32),
+                pltpu.SemaphoreType.DMA((edge_x // CHUNK + 1,)),
+            ],
+        )(*found)
 
     in_specs = (
         P(("grp", "slab"), None),

time: 37.6 us -> 28 us (0.74)
  Pallas kernels: 33.8 us -> 27.2 us
  local copies, waits for them, and re-layouts: 2.95 us -> 0 us
    pallas_call x1 -> x2, Pallas kernels: 33.8 us -> 27.2 us  [the longest x1 25.1 us: body(): pl.pallas_call(functools.partial(exchange, groups, slabs), out_shape=(jax...]
    unnamed x2 -> x0, local copies, waits for them, and re-layouts: 2.95 us -> none
where the time goes in v2:
time: 28 us; the launch traced here: 27.9 us
  Pallas kernels  27.2 us (97%)
  between operations  0.64 us (2%)
    pallas_call x1, Pallas kernels, body(): pl.pallas_call(functools.partial(exchange, groups, slabs), out_shape=(jax...  25.1 us
    pallas_call x1, Pallas kernels, body(): pl.pallas_call(finish, out_shape=(jax.ShapeDtypeStruct(field.shape, f32),...  2.08 us

profile of v2, /device:TPU:1, one launch (start us, length us, event | category | flops | bytes accessed | tf_op | source)
XLA Modules:
  0.0 27.9 jit_solution(5648249524259658254)
XLA Ops:
  0.6 25.1 %shard_map.104 = (f32[2,512]{1,0:T(2,128)}, f32[512,128]{1,0:T(8,128)}, f32[72,384]{1,0:T(8,128)}, f32[512,128]{1,0:T(8,128)}, f32[512,128]{1,0:T(8,128)}, /*index=5*/f32[64,128]{1,0:T(8,128)}, f32[64,128]{1,0:T(8,128)}) custom-call(f32[2,512]{1,0:T(2,128)} %field_any.1, f32[1,128]{1,0:T(1,128)} %kappa_any.1, f32[2,512]{1,0:T(2,128)} %heat_any.1, ...), custom_call_target="tpu_custom_call" | custom-call | tf_op jit(solution)/shard_map/pallas_call | solution.py:616
  25.8 2.1 %shard_map.105 = (f32[2,512]{1,0:T(2,128)}, f32[512,128]{1,0:T(8,128)}) custom-call(f32[2,512]{1,0:T(2,128)} %get-tuple-element.9.field_ref, f32[512,128]{1,0:T(8,128)} %get-tuple-element.10.solid_ref, f32[72,384]{1,0:T(8,128)} %get-tuple-element.11.planes, f32[512,128]{1,0:T(8,128)} %get-tuple-element.12.gathered, f32[512,128]{1,0:T(8,128)} %get-tuple-element.13.nucleation, ...), custom_call_target="tpu_custom_call" | custom-call | tf_op jit(solution)/shard_map/pallas_call | solution.py:672

commit v3 on v2

--- a/solution.py
+++ b/solution.py
@@ -239,8 +239,13 @@
     from_ahead_y,
     from_behind_y,
     tally,
+    edge_low,
+    edge_high,
     load_sems,
     box_sems,
+    row_sems,
+    forward_sems,
+    ready_sem,
     near_sems,
     near_send_sems,
     edge_recv_sems,
@@ -267,26 +272,69 @@
     h = lax.axis_index("slab")
     g_next = lax.rem(g + 1, groups)
     g_prev = lax.rem(g + groups - 1, groups)
-    high_edge = h >= slabs - 2
-    low_edge = h <= 2
+
+    ordered = g == groups - 1
+
+    def place(rank):
+        fold = rank >> 3
+        row = jnp.where((fold & 1) == 1, (fold + 1) >> 1, (0 - (fold >> 1)) & (slabs // 8 - 1))
+        return 8 * row + (rank & 7)
+
+    def rank_of(other):
+        row = other >> 3
+        fold = jnp.where(
+            row == 0, 0, jnp.where(row <= slabs // 16, 2 * row - 1, slabs // 4 - 2 * row)
+        )
+        return 8 * fold + (other & 7)
+
+    rank = rank_of(h)
+    prev_upper = g == 0
+    at_low, at_high = h <= 2, h >= slabs - 2
+    sends_low = at_low & (g > 0) & jnp.logical_not(ordered)
+    sends_high = at_high
 
     barrier = pltpu.get_barrier_semaphore()
 
     def greet(to_g, to_h):
         pl.semaphore_signal(barrier, inc=1, device_id=(to_g, to_h), device_id_type=MESH)
 
-    greet(g_prev, jnp.int32(slabs - 2))
-    greet(g_prev, jnp.int32(slabs - 1))
-    for first in range(3):
-        greet(g_next, jnp.int32(first))
     greet(g_prev, h)
-    greet(g_next, h)
-
-    def greet_group(step, carry):
-        greet(g, lax.rem(h + 1 + step, slabs))
+    for last in range(2):
+        greet(g_prev, jnp.int32(slabs - 1 - last))
+
+    @pl.when(jnp.logical_not(ordered))
+    def _():
+        greet(g_next, h)
+
+    @pl.when(g < groups - 2)
+    def _():
+        for first in range(3):
+            greet(g_next, jnp.int32(first))
+
+    here = g * slabs + h
+    count = groups * slabs
+    near_to = {}
+    for by in (1, -1, 2, -2):
+        there = lax.rem(here + by + count, count)
+        to_g, to_h = there // slabs, lax.rem(there, slabs)
+        inside = to_g == g
+        upper = jnp.where(
+            inside, ordered & (rank_of(to_h) > rank), prev_upper if by < 0 else False
+        )
+        silent = ordered if by > 0 else False
+
+        @pl.when(jnp.logical_not(inside | silent))
+        def _(to_g=to_g, to_h=to_h):
+            greet(to_g, to_h)
+
+        near_to[by] = (to_g, to_h, inside, upper)
+
+    def greet_rank(r, carry):
+        greet(g, place(r))
         return carry
 
-    lax.fori_loop(0, slabs - 1, greet_group, 0)
+    lax.fori_loop(0, jnp.where(ordered, 0, rank), greet_rank, 0)
+    lax.fori_loop(rank + 1, slabs, greet_rank, 0)
 
     for copy in loads[:3]:
         copy.wait()
@@ -312,6 +360,81 @@
             kappa_lane, take_lanes(kappa_rows, index), windows(shifted_heat, m)
         )
 
+    expected = (
+        jnp.where(ordered, rank, slabs - 1)
+        + jnp.where(g > 0, 2, 1)
+        + jnp.where(sends_low, slabs, 0)
+        + jnp.where(sends_high, slabs, 0)
+    )
+    for to_g, to_h, inside, upper in near_to.values():
+        expected = expected + jnp.where(jnp.logical_not(inside | upper), 1, 0)
+
+    @pl.when(ordered)
+    def _():
+        pl.semaphore_wait(barrier, expected)
+
+    def remote(source, target, send_sem, recv_sem, device):
+        return pltpu.make_async_remote_copy(
+            src_ref=source,
+            dst_ref=target,
+            send_sem=send_sem,
+            recv_sem=recv_sem,
+            device_id=device,
+            device_id_type=MESH,
+        )
+
+    def start_if(condition, copy):
+        @pl.when(condition)
+        def _():
+            copy.start()
+
+    def wait_messages(many, sem):
+        size = tally.at[pl.ds(0, many)]
+        pltpu.make_async_copy(size, size, sem).wait()
+
+    def post(device, target_row, send_sem, recv_sem):
+        return remote(
+            outbox.at[pl.ds(device[1], 1), :],
+            inbox.at[pl.ds(target_row, 1), :],
+            send_sem,
+            recv_sem,
+            device,
+        )
+
+    near = {}
+    for by in (1, -1, 2, -2):
+        to_g, to_h, inside, upper = near_to[by]
+        slot = {2: 0, 1: 1, -1: 2, -2: 3}[by]
+        pairs = [(field_ref, near_field, slot, 0)]
+        if by in (1, -1):
+            pairs.append((heat_ref, near_heat, slot - 1, 1))
+        if by != -2:
+            pairs.append((kappa_ref, near_kappa, slot, 2))
+        near[by] = [
+            remote(
+                source,
+                target.at[place_],
+                near_send_sems.at[slot, kind],
+                near_sems.at[slot, kind],
+                (to_g, to_h),
+            )
+            for source, target, place_, kind in pairs
+        ]
+        for copy in near[by]:
+            start_if(ordered & jnp.logical_not(upper), copy)
+
+    slot_low = jnp.minimum(h, 2) + 2
+    slot_high = jnp.maximum(h - (slabs - 2), 0)
+
+    def fan_high():
+        def body(to_h, carry):
+            post((g_next, to_h), slot_high, box_sems.at[1], row_sems.at[slot_high]).start()
+            return carry
+
+        lax.fori_loop(0, slabs, body, 0)
+
+    pl.when(ordered & sends_high)(fan_high)
+
     for copy in loads[3:]:
         copy.wait()
     weight = 1 << (2 * lax.broadcasted_iota(jnp.int32, (6, 1), 0))
@@ -324,6 +447,16 @@
         )
     rest = jnp.concatenate([codes[:, 7936:8000], jnp.zeros((1, 64), jnp.int32)], 1)
     words[248:256, :] = jnp.broadcast_to(rest, (8, 128))
+
+    edge_x = solid_ref.shape[0]
+
+    def weighted_by(code, solid, d):
+        return (0.25 * solid) * (((code >> (2 * d)) & 3) + 1).astype(jnp.float32)
+
+    edge_low[...] = weighted_by(lookup(words, label_ref[0:8, :]), solid_ref[0:8, :], 0)
+    edge_high[...] = weighted_by(
+        lookup(words, label_ref[edge_x - 8 : edge_x, :]), solid_ref[edge_x - 8 : edge_x, :], 1
+    )
 
     lane_c = lax.broadcasted_iota(jnp.int32, (CHUNK, 128), 1)
     depth = lane_c & 15
@@ -360,76 +493,57 @@
 
     ahead_y[...] = jnp.zeros(ahead_y.shape, jnp.float32)
     behind_y[...] = jnp.zeros(behind_y.shape, jnp.float32)
-    edge_x = solid_ref.shape[0]
     chunks = edge_x // CHUNK
-    x, y = lax.rem(h // 2, 4), h // 8
-    hops = jnp.abs(x - 2) + jnp.abs(y - 4)
-    ahead = jnp.where(g == 0, chunks, jnp.minimum(2 * hops, chunks))
+    hops = jnp.abs(lax.rem(h // 2, 4) - 2) + jnp.abs(h // 8 - 4)
+    ahead = jnp.where(g == 0, chunks, jnp.where(ordered, 0, jnp.minimum(2 * hops, chunks)))
     lax.fori_loop(0, ahead, cells, 0)
 
-    expected = 63 + 2 + jnp.where(high_edge, slabs, 0) + jnp.where(low_edge, slabs, 0)
-    pl.semaphore_wait(barrier, expected)
-
-    def post(to_g, to_h, row):
-        return pltpu.make_async_remote_copy(
-            src_ref=outbox.at[pl.ds(to_h, 1), :],
-            dst_ref=inbox.at[pl.ds(row, 1), :],
-            send_sem=box_sems.at[0],
-            recv_sem=box_sems.at[1],
-            device_id=(to_g, to_h),
-            device_id_type=MESH,
-        )
-
-    def wait_messages(many, kind):
-        size = tally.at[pl.ds(0, many)]
-        pltpu.make_async_copy(size, size, box_sems.at[kind]).wait()
-
-    here = g * slabs + h
-    count = groups * slabs
-    near = []
+    @pl.when(jnp.logical_not(ordered))
+    def _():
+        pl.semaphore_wait(barrier, expected)
+
+    to_prev = remote(edge_low, from_ahead_x, edge_send_sems.at[2], edge_recv_sems.at[2], (g_prev, h))
+    to_next = remote(edge_high, from_behind_x, edge_send_sems.at[3], edge_recv_sems.at[3], (g_next, h))
+    start_if(jnp.logical_not(prev_upper), to_prev)
+    to_next.start()
+
     for by in (1, -1, 2, -2):
-        there = lax.rem(here + by + count, count)
-        device = (there // slabs, lax.rem(there, slabs))
-        slot = {2: 0, 1: 1, -1: 2, -2: 3}[by]
-        pairs = [(field_ref, near_field, slot, 0)]
-        if by in (1, -1):
-            pairs.append((heat_ref, near_heat, slot - 1, 1))
-        if by != -2:
-            pairs.append((kappa_ref, near_kappa, slot, 2))
-        for source, target, place, kind in pairs:
-            copy = pltpu.make_async_remote_copy(
-                src_ref=source,
-                dst_ref=target.at[place],
-                send_sem=near_send_sems.at[slot, kind],
-                recv_sem=near_sems.at[slot, kind],
-                device_id=device,
-                device_id_type=MESH,
-            )
-            copy.start()
-            near.append(copy)
-
-    def post_group(step, carry):
-        to_h = lax.rem(h + 1 + step, slabs)
-        post(g, to_h, h + 2).start()
+        for copy in near[by]:
+            start_if(jnp.logical_not(ordered | near_to[by][3]), copy)
+
+    @pl.when(sends_low)
+    def _():
+        def body(to_h, carry):
+            post((g_prev, to_h), slabs + slot_low, box_sems.at[1], row_sems.at[slot_low]).start()
+            return carry
+
+        lax.fori_loop(0, slabs, body, 0)
+
+    pl.when(jnp.logical_not(ordered) & sends_high)(fan_high)
+
+    kind = jnp.where(at_low, 3, 2)
+    own = pltpu.make_async_copy(
+        outbox.at[pl.ds(h, 1), :], inbox.at[pl.ds(h + 2, 1), :], box_sems.at[kind]
+    )
+    own.start()
+
+    def post_group(r, carry):
+        post((g, place(r)), h + 2, box_sems.at[0], box_sems.at[kind]).start()
         return carry
 
-    @pl.when(high_edge)
-    def _():
-        def body(to_h, carry):
-            post(g_next, to_h, h - (slabs - 2)).start()
-            return carry
-
-        lax.fori_loop(0, slabs, body, 0)
-
-    @pl.when(low_edge)
-    def _():
-        def body(to_h, carry):
-            post(g_prev, to_h, h + slabs + 2).start()
-            return carry
-
-        lax.fori_loop(0, slabs, body, 0)
-
-    lax.fori_loop(0, slabs - 1, post_group, 0)
+    def answer(r, carry):
+        pl.semaphore_signal(
+            ready_sem, inc=1, device_id=(g, place(r)), device_id_type=MESH
+        )
+        return carry
+
+    def post_above(step, carry):
+        post((g, place(slabs - 1 - step)), h + 2, box_sems.at[0], box_sems.at[kind]).start()
+        return carry
+
+    lax.fori_loop(0, jnp.where(ordered, rank, 0), answer, 0)
+    lax.fori_loop(0, jnp.where(ordered, 0, slabs - 1 - rank), post_above, 0)
+    lax.fori_loop(0, rank, post_group, 0)
 
     lax.fori_loop(ahead, chunks, cells, 0)
 
@@ -452,31 +566,74 @@
 
     h_next = lax.rem(h + 1, slabs)
     h_prev = lax.rem(h + slabs - 1, slabs)
-    edges = []
-    for number, (source, target, device) in enumerate(
-        (
-            (ahead_y, from_ahead_y, (g, h_prev)),
-            (behind_y, from_behind_y, (g, h_next)),
-            (ahead_x.at[0:8, :], from_ahead_x, (g_prev, h)),
-            (behind_x.at[edge_x - 8 : edge_x, :], from_behind_x, (g_next, h)),
-        )
-    ):
-        copy = pltpu.make_async_remote_copy(
-            src_ref=source,
-            dst_ref=target,
-            send_sem=edge_send_sems.at[number],
-            recv_sem=edge_recv_sems.at[number],
-            device_id=device,
-            device_id_type=MESH,
-        )
-        copy.start()
-        edges.append(copy)
+    down_y_copy = remote(
+        ahead_y, from_ahead_y, edge_send_sems.at[0], edge_recv_sems.at[0], (g, h_prev)
+    )
+    up_y_copy = remote(
+        behind_y, from_behind_y, edge_send_sems.at[1], edge_recv_sems.at[1], (g, h_next)
+    )
+
+    prev_above = ordered & (rank_of(h_prev) > rank)
+    next_above = ordered & (rank_of(h_next) > rank)
+    start_if(jnp.logical_not(prev_above), down_y_copy)
+    start_if(jnp.logical_not(next_above), up_y_copy)
 
     gathered[0 : edge_x - 1, :] = gathered[0 : edge_x - 1, :] + ahead_x[1:edge_x, :]
     gathered[1:edge_x, :] = gathered[1:edge_x, :] + behind_x[0 : edge_x - 1, :]
 
-    for copy in near:
-        copy.wait_recv()
+    @pl.when(ordered & (rank < slabs - 1))
+    def _():
+        pl.semaphore_wait(ready_sem, slabs - 1 - rank)
+
+    lax.fori_loop(0, jnp.where(ordered, slabs - 1 - rank, 0), post_above, 0)
+    start_if(prev_above, down_y_copy)
+    start_if(next_above, up_y_copy)
+    for by in (1, -1, 2, -2):
+        to_g, to_h, inside, upper = near_to[by]
+        for copy in near[by]:
+            start_if(upper & inside, copy)
+
+    wait_messages(3, box_sems.at[3])
+
+    to_prev_rows = [
+        remote(
+            inbox.at[pl.ds(2 + k, 1), :],
+            inbox.at[pl.ds(slabs + 2 + k, 1), :],
+            forward_sems.at[k],
+            row_sems.at[2 + k],
+            (g_prev, h),
+        )
+        for k in range(3)
+    ]
+    for copy in to_prev_rows:
+        start_if(ordered, copy)
+    wait_messages(slabs - 3, box_sems.at[2])
+
+    for by in (1, -1, 2, -2):
+        to_g, to_h, inside, upper = near_to[by]
+
+        @pl.when(upper & jnp.logical_not(inside))
+        def _(by=by):
+            for copy in near[-by]:
+                copy.wait_recv()
+            for copy in near[by]:
+                copy.start()
+
+    @pl.when(prev_upper)
+    def _():
+        to_next.wait_recv()
+        to_prev.start()
+
+    for copy in to_prev_rows:
+        start_if(prev_upper, copy)
+
+    for by in (1, -1, 2, -2):
+
+        @pl.when(near_to[-by][2] | jnp.logical_not(near_to[-by][3]))
+        def _(by=by):
+            for copy in near[by]:
+                copy.wait_recv()
+
     zero = jnp.zeros((8, 128), jnp.float32)
     stacked_field = jnp.stack(
         [
@@ -514,8 +671,8 @@
     for q in range(4):
         new_field_ref[:, 128 * q : 128 * q + 128] = moved[2 * q : 2 * q + 2, :]
 
-    inbox[pl.ds(h + 2, 1), :] = outbox[pl.ds(h, 1), :]
-    wait_messages(slabs + 4, 1)
+    for number in range(5):
+        wait_messages(1, row_sems.at[number])
     shifts = BrickShifts((ROWS, 128))
     box_lane = lax.broadcasted_iota(jnp.int32, (ROWS, 128), 1)
     half = box_lane & 63
@@ -533,22 +690,35 @@
     planes[:, 0:256] = pair
     planes[:, 256:384] = pltpu.roll(pair[:, 0:128], ROWS - 1, 0)
 
-    for copy in edges:
-        copy.wait_recv()
+    down_y_copy.wait_recv()
+    up_y_copy.wait_recv()
+
+    to_prev.wait_recv()
+
+    @pl.when(jnp.logical_not(prev_upper))
+    def _():
+        to_next.wait_recv()
+
     gathered[edge_x - 1 : edge_x, :] = gathered[edge_x - 1 : edge_x, :] + from_ahead_x[0:1, :]
     gathered[0:1, :] = gathered[0:1, :] + from_behind_x[7:8, :]
     side_ahead[...] = from_ahead_y[...]
     side_behind[...] = from_behind_y[...]
 
-    for copy in near + edges:
+    for copies in near.values():
+        for copy in copies:
+            copy.wait_send()
+    for copy in (down_y_copy, up_y_copy, to_prev, to_next):
         copy.wait_send()
-    @pl.when(high_edge | low_edge)
-    def _():
-        wait_messages(2 * slabs - 1, 0)
-
-    @pl.when(jnp.logical_not(high_edge | low_edge))
-    def _():
-        wait_messages(slabs - 1, 0)
+    wait_messages(slabs - 1, box_sems.at[0])
+
+    @pl.when(sends_low | sends_high)
+    def _():
+        wait_messages(slabs, box_sems.at[1])
+
+    @pl.when(prev_upper | ordered)
+    def _():
+        for copy in to_prev_rows:
+            copy.wait_send()
 
 
 def finish(
@@ -624,7 +794,7 @@
                 jax.ShapeDtypeStruct((CHUNK, 128), f32),
                 jax.ShapeDtypeStruct((CHUNK, 128), f32),
             ),
-            in_specs=[anywhere] * 9,
+            in_specs=[pl.BlockSpec(memory_space=pltpu.HBM)] * 9,
             out_specs=(vmem,) * 7,
             scratch_shapes=[
                 pltpu.VMEM(field.shape, f32),
@@ -649,25 +819,37 @@
                 pltpu.VMEM((8, 128), f32),
                 pltpu.VMEM((CHUNK, 128), f32),
                 pltpu.VMEM((CHUNK, 128), f32),
-                pltpu.VMEM((2 * slabs, 2, 128), f32),
+                pltpu.VMEM((slabs, 2, 128), f32),
+                pltpu.VMEM((8, 128), f32),
+                pltpu.VMEM((8, 128), f32),
                 pltpu.SemaphoreType.DMA((9,)),
-                pltpu.SemaphoreType.DMA((2,)),
+                pltpu.SemaphoreType.DMA((4,)),
+                pltpu.SemaphoreType.DMA((5,)),
+                pltpu.SemaphoreType.DMA((3,)),
+                pltpu.SemaphoreType.REGULAR,
                 pltpu.SemaphoreType.DMA((4, 3)),
                 pltpu.SemaphoreType.DMA((4, 3)),
                 pltpu.SemaphoreType.DMA((4,)),
                 pltpu.SemaphoreType.DMA((4,)),
             ],
-            compiler_params=pltpu.CompilerParams(collective_id=0, has_side_effects=True),
+            compiler_params=pltpu.CompilerParams(
+                collective_id=0, has_side_effects=True, vmem_limit_bytes=16 << 20
+            ),
         )(
-            field,
-            kappa,
-            heat,
-            solid,
-            label,
-            table.T,
-            slot.reshape(2, 128),
-            seed.reshape(2, 128),
-            jnp.asarray(matrix),
+            *(
+                pltpu.with_memory_space_constraint(value, pltpu.HBM)
+                for value in (
+                    field,
+                    kappa,
+                    heat,
+                    solid,
+                    label,
+                    table.T,
+                    slot.reshape(2, 128),
+                    seed.reshape(2, 128),
+                    jnp.asarray(matrix),
+                )
+            )
         )
         return pl.pallas_call(
             finish,
@@ -681,6 +863,7 @@
                 pltpu.VMEM(cells, f32),
                 pltpu.SemaphoreType.DMA((edge_x // CHUNK + 1,)),
             ],
+            compiler_params=pltpu.CompilerParams(vmem_limit_bytes=16 << 20),
         )(*found)
 
     in_specs = (

time: 28 us -> 22.4 us (0.80)
  Pallas kernels: 27.2 us -> 21.6 us
    pallas_call x1, Pallas kernels: 25.1 us -> 20.7 us  [body(): pl.pallas_call(functools.partial(exchange, groups, slabs), out_shape=(jax...]
    pallas_call x1, Pallas kernels: 2.08 us -> 0.94 us  [body(): pl.pallas_call(finish, out_shape=(jax.ShapeDtypeStruct(field.shape, f32),...]
where the time goes in v3:
time: 22.4 us; the launch traced here: 22.2 us
  Pallas kernels  21.6 us (96%)
  between operations  0.64 us (3%)
    pallas_call x1, Pallas kernels, body(): pl.pallas_call(functools.partial(exchange, groups, slabs), out_shape=(jax...  20.7 us
    pallas_call x1, Pallas kernels, body(): pl.pallas_call(finish, out_shape=(jax.ShapeDtypeStruct(field.shape, f32),...  0.94 us

profile of v3, /device:TPU:1, one launch (start us, length us, event | category | flops | bytes accessed | tf_op | source)
XLA Modules:
  0.0 22.2 jit_solution(14863045003784311146)
XLA Ops:
  0.6 20.7 %shard_map.104 = (f32[2,512]{1,0:T(2,128)S(1)}, f32[512,128]{1,0:T(8,128)S(1)}, f32[72,384]{1,0:T(8,128)S(1)}, f32[512,128]{1,0:T(8,128)S(1)}, f32[512,128]{1,0:...) custom-call(f32[2,512]{1,0:T(2,128)} %field_any.1, f32[1,128]{1,0:T(1,128)} %kappa_any.1, f32[2,512]{1,0:T(2,128)} %heat_any.1, ...), custom_call_target="tpu_custom_call" | custom-call | tf_op jit(solution)/shard_map/pallas_call | solution.py:786
  21.3 0.9 %shard_map.105 = (f32[2,512]{1,0:T(2,128)}, f32[512,128]{1,0:T(8,128)}) custom-call(f32[2,512]{1,0:T(2,128)S(1)} %get-tuple-element.9.field_ref, f32[512,128]{1,0:T(8,128)S(1)} %get-tuple-element.10.solid_ref, f32[72,384]{1,0:T(8,128)S(1)} %get-tuple-element.11.planes, f32[512,128]{1,0:T(8,128)S(1)} %get-tuple-element.12.gathered, ...), custom_call_target="tpu_custom_call" | custom-call | tf_op jit(solution)/shard_map/pallas_call | solution.py:854

commit v4 on v3

--- a/solution.py
+++ b/solution.py
@@ -275,17 +275,24 @@
 
     ordered = g == groups - 1
 
+    rows_y = slabs // 8
+    early = 22
+
     def place(rank):
-        fold = rank >> 3
-        row = jnp.where((fold & 1) == 1, (fold + 1) >> 1, (0 - (fold >> 1)) & (slabs // 8 - 1))
-        return 8 * row + (rank & 7)
+        at = jnp.where(rank < 2, rank + early, jnp.where(rank < early + 2, rank - 2, rank))
+        fold = at >> 3
+        row = jnp.where((fold & 1) == 1, (fold + 1) >> 1, 0 - (fold >> 1)) & (rows_y - 1)
+        return 8 * row + (at & 7)
 
     def rank_of(other):
         row = other >> 3
         fold = jnp.where(
-            row == 0, 0, jnp.where(row <= slabs // 16, 2 * row - 1, slabs // 4 - 2 * row)
-        )
-        return 8 * fold + (other & 7)
+            row == 0, 0, jnp.where(row <= rows_y // 2, 2 * row - 1, 2 * (rows_y - row))
+        )
+        at = 8 * fold + (other & 7)
+        return jnp.where(
+            other >= slabs - 2, other - (slabs - 2), jnp.where(at < early, at + 2, at)
+        )
 
     rank = rank_of(h)
     prev_upper = g == 0
@@ -369,7 +376,9 @@
     for to_g, to_h, inside, upper in near_to.values():
         expected = expected + jnp.where(jnp.logical_not(inside | upper), 1, 0)
 
-    @pl.when(ordered)
+    first = ordered & sends_high
+
+    @pl.when(first)
     def _():
         pl.semaphore_wait(barrier, expected)
 
@@ -421,7 +430,7 @@
             for source, target, place_, kind in pairs
         ]
         for copy in near[by]:
-            start_if(ordered & jnp.logical_not(upper), copy)
+            start_if(first & jnp.logical_not(upper), copy)
 
     slot_low = jnp.minimum(h, 2) + 2
     slot_high = jnp.maximum(h - (slabs - 2), 0)
@@ -433,7 +442,7 @@
 
         lax.fori_loop(0, slabs, body, 0)
 
-    pl.when(ordered & sends_high)(fan_high)
+    pl.when(first)(fan_high)
 
     for copy in loads[3:]:
         copy.wait()
@@ -494,11 +503,19 @@
     ahead_y[...] = jnp.zeros(ahead_y.shape, jnp.float32)
     behind_y[...] = jnp.zeros(behind_y.shape, jnp.float32)
     chunks = edge_x // CHUNK
-    hops = jnp.abs(lax.rem(h // 2, 4) - 2) + jnp.abs(h // 8 - 4)
-    ahead = jnp.where(g == 0, chunks, jnp.where(ordered, 0, jnp.minimum(2 * hops, chunks)))
+    x, y = (h >> 1) & 3, h >> 3
+    hops = jnp.abs(x - 2) + jnp.abs(y - 4)
+    last_ahead = jnp.maximum(chunks - 2 * x - jnp.where(y >= 4, 4, 0), 0)
+    ahead = jnp.where(
+        g == 0,
+        chunks,
+        jnp.where(
+            first, 0, jnp.where(ordered, last_ahead, jnp.minimum(2 * hops, chunks))
+        ),
+    )
     lax.fori_loop(0, ahead, cells, 0)
 
-    @pl.when(jnp.logical_not(ordered))
+    @pl.when(jnp.logical_not(first))
     def _():
         pl.semaphore_wait(barrier, expected)
 
@@ -509,7 +526,7 @@
 
     for by in (1, -1, 2, -2):
         for copy in near[by]:
-            start_if(jnp.logical_not(ordered | near_to[by][3]), copy)
+            start_if(jnp.logical_not(first | near_to[by][3]), copy)
 
     @pl.when(sends_low)
     def _():
@@ -619,14 +636,6 @@
             for copy in near[by]:
                 copy.start()
 
-    @pl.when(prev_upper)
-    def _():
-        to_next.wait_recv()
-        to_prev.start()
-
-    for copy in to_prev_rows:
-        start_if(prev_upper, copy)
-
     for by in (1, -1, 2, -2):
 
         @pl.when(near_to[-by][2] | jnp.logical_not(near_to[-by][3]))
@@ -670,6 +679,14 @@
     )[2]
     for q in range(4):
         new_field_ref[:, 128 * q : 128 * q + 128] = moved[2 * q : 2 * q + 2, :]
+
+    @pl.when(prev_upper)
+    def _():
+        to_next.wait_recv()
+        to_prev.start()
+
+    for copy in to_prev_rows:
+        start_if(prev_upper, copy)
 
     for number in range(5):
         wait_messages(1, row_sems.at[number])

time: 22.4 us -> 21.8 us (0.973)
  Pallas kernels: 21.6 us -> 21 us
    pallas_call x1, Pallas kernels: 20.7 us -> 20.1 us  [body(): pl.pallas_call(functools.partial(exchange, groups, slabs), out_shape=(jax...]
where the time goes in v4:
time: 21.8 us; the launch traced here: 21.7 us
  Pallas kernels  21 us (96%)
  between operations  0.64 us (3%)
    pallas_call x1, Pallas kernels, body(): pl.pallas_call(functools.partial(exchange, groups, slabs), out_shape=(jax...  20.1 us
    pallas_call x1, Pallas kernels, body(): pl.pallas_call(finish, out_shape=(jax.ShapeDtypeStruct(field.shape, f32),...  0.94 us

profile of v4, /device:TPU:1, one launch (start us, length us, event | category | flops | bytes accessed | tf_op | source)
XLA Modules:
  0.0 21.7 jit_solution(11894925991402386393)
XLA Ops:
  0.6 20.1 %shard_map.104 = (f32[2,512]{1,0:T(2,128)S(1)}, f32[512,128]{1,0:T(8,128)S(1)}, f32[72,384]{1,0:T(8,128)S(1)}, f32[512,128]{1,0:T(8,128)S(1)}, f32[512,128]{1,0:...) custom-call(f32[2,512]{1,0:T(2,128)} %field_any.1, f32[1,128]{1,0:T(1,128)} %kappa_any.1, f32[2,512]{1,0:T(2,128)} %heat_any.1, ...), custom_call_target="tpu_custom_call" | custom-call | tf_op jit(solution)/shard_map/pallas_call | solution.py:803
  20.7 0.9 %shard_map.105 = (f32[2,512]{1,0:T(2,128)}, f32[512,128]{1,0:T(8,128)}) custom-call(f32[2,512]{1,0:T(2,128)S(1)} %get-tuple-element.9.field_ref, f32[512,128]{1,0:T(8,128)S(1)} %get-tuple-element.10.solid_ref, f32[72,384]{1,0:T(8,128)S(1)} %get-tuple-element.11.planes, f32[512,128]{1,0:T(8,128)S(1)} %get-tuple-element.12.gathered, ...), custom_call_target="tpu_custom_call" | custom-call | tf_op jit(solution)/shard_map/pallas_call | solution.py:871

commit v5 on v4

--- a/solution.py
+++ b/solution.py
@@ -244,26 +244,28 @@
     load_sems,
     box_sems,
     row_sems,
-    forward_sems,
+    forward_sem,
     ready_sem,
     near_sems,
     near_send_sems,
     edge_recv_sems,
     edge_send_sems,
 ):
+    def wait_messages(many, sem):
+        size = tally.at[pl.ds(0, many)]
+        pltpu.make_async_copy(size, size, sem).wait()
+
     loads = []
-    for number, (source, target) in enumerate(
-        (
-            (field_any, field_ref),
-            (heat_any, heat_ref),
-            (kappa_any, kappa_ref),
-            (table_any, table_ref),
-            (label_any, label_ref),
-            (solid_any, solid_ref),
-            (slot_any, slot_ref),
-            (seed_any, seed_ref),
-            (matrix_any, matrix_ref),
-        )
+    for source, target, number in (
+        (field_any, field_ref, 0),
+        (heat_any, heat_ref, 0),
+        (kappa_any, kappa_ref, 1),
+        (table_any, table_ref, 2),
+        (label_any, label_ref, 3),
+        (solid_any, solid_ref, 4),
+        (slot_any, slot_ref, 5),
+        (seed_any, seed_ref, 5),
+        (matrix_any, matrix_ref, 6),
     ):
         copy = pltpu.make_async_copy(source, target, load_sems.at[number])
         copy.start()
@@ -343,8 +345,8 @@
     lax.fori_loop(0, jnp.where(ordered, 0, rank), greet_rank, 0)
     lax.fori_loop(rank + 1, slabs, greet_rank, 0)
 
-    for copy in loads[:3]:
-        copy.wait()
+    wait_messages(8, load_sems.at[0])
+    loads[2].wait()
     sub = lax.broadcasted_iota(jnp.int32, (8, 128), 0)
     lane = lax.broadcasted_iota(jnp.int32, (8, 128), 1)
     window = 8 * sub + (lane & 63)
@@ -396,10 +398,6 @@
         @pl.when(condition)
         def _():
             copy.start()
-
-    def wait_messages(many, sem):
-        size = tally.at[pl.ds(0, many)]
-        pltpu.make_async_copy(size, size, sem).wait()
 
     def post(device, target_row, send_sem, recv_sem):
         return remote(
@@ -423,8 +421,8 @@
             remote(
                 source,
                 target.at[place_],
-                near_send_sems.at[slot, kind],
-                near_sems.at[slot, kind],
+                near_send_sems.at[kind // 2],
+                near_sems.at[(0, 4, 6)[kind] + place_],
                 (to_g, to_h),
             )
             for source, target, place_, kind in pairs
@@ -437,15 +435,16 @@
 
     def fan_high():
         def body(to_h, carry):
-            post((g_next, to_h), slot_high, box_sems.at[1], row_sems.at[slot_high]).start()
+            post((g_next, to_h), slot_high, box_sems.at[1], row_sems.at[0]).start()
             return carry
 
         lax.fori_loop(0, slabs, body, 0)
 
     pl.when(first)(fan_high)
 
-    for copy in loads[3:]:
+    for copy in (*loads[3:6], loads[8]):
         copy.wait()
+    wait_messages(2, load_sems.at[5])
     weight = 1 << (2 * lax.broadcasted_iota(jnp.int32, (6, 1), 0))
     codes = jnp.sum((table_ref[...] - 1) * weight, axis=0, keepdims=True)
     for row in range(31):
@@ -519,8 +518,8 @@
     def _():
         pl.semaphore_wait(barrier, expected)
 
-    to_prev = remote(edge_low, from_ahead_x, edge_send_sems.at[2], edge_recv_sems.at[2], (g_prev, h))
-    to_next = remote(edge_high, from_behind_x, edge_send_sems.at[3], edge_recv_sems.at[3], (g_next, h))
+    to_prev = remote(edge_low, from_ahead_x, edge_send_sems.at[1], edge_recv_sems.at[2], (g_prev, h))
+    to_next = remote(edge_high, from_behind_x, edge_send_sems.at[1], edge_recv_sems.at[3], (g_next, h))
     start_if(jnp.logical_not(prev_upper), to_prev)
     to_next.start()
 
@@ -531,7 +530,7 @@
     @pl.when(sends_low)
     def _():
         def body(to_h, carry):
-            post((g_prev, to_h), slabs + slot_low, box_sems.at[1], row_sems.at[slot_low]).start()
+            post((g_prev, to_h), slabs + slot_low, box_sems.at[1], row_sems.at[1]).start()
             return carry
 
         lax.fori_loop(0, slabs, body, 0)
@@ -587,7 +586,7 @@
         ahead_y, from_ahead_y, edge_send_sems.at[0], edge_recv_sems.at[0], (g, h_prev)
     )
     up_y_copy = remote(
-        behind_y, from_behind_y, edge_send_sems.at[1], edge_recv_sems.at[1], (g, h_next)
+        behind_y, from_behind_y, edge_send_sems.at[0], edge_recv_sems.at[1], (g, h_next)
     )
 
     prev_above = ordered & (rank_of(h_prev) > rank)
@@ -616,8 +615,8 @@
         remote(
             inbox.at[pl.ds(2 + k, 1), :],
             inbox.at[pl.ds(slabs + 2 + k, 1), :],
-            forward_sems.at[k],
-            row_sems.at[2 + k],
+            forward_sem,
+            row_sems.at[1],
             (g_prev, h),
         )
         for k in range(3)
@@ -688,8 +687,8 @@
     for copy in to_prev_rows:
         start_if(prev_upper, copy)
 
-    for number in range(5):
-        wait_messages(1, row_sems.at[number])
+    wait_messages(2, row_sems.at[0])
+    wait_messages(3, row_sems.at[1])
     shifts = BrickShifts((ROWS, 128))
     box_lane = lax.broadcasted_iota(jnp.int32, (ROWS, 128), 1)
     half = box_lane & 63
@@ -721,11 +720,10 @@
     side_ahead[...] = from_ahead_y[...]
     side_behind[...] = from_behind_y[...]
 
-    for copies in near.values():
-        for copy in copies:
-            copy.wait_send()
-    for copy in (down_y_copy, up_y_copy, to_prev, to_next):
-        copy.wait_send()
+    wait_messages(24, near_send_sems.at[0])
+    pltpu.make_async_copy(near_kappa, near_kappa, near_send_sems.at[1]).wait()
+    wait_messages(64, edge_send_sems.at[0])
+    wait_messages(8, edge_send_sems.at[1])
     wait_messages(slabs - 1, box_sems.at[0])
 
     @pl.when(sends_low | sends_high)
@@ -734,8 +732,7 @@
 
     @pl.when(prev_upper | ordered)
     def _():
-        for copy in to_prev_rows:
-            copy.wait_send()
+        wait_messages(3, forward_sem)
 
 
 def finish(
@@ -752,7 +749,7 @@
     sems,
 ):
     chunks = solid_ref.shape[0] // CHUNK
-    field_out = pltpu.make_async_copy(field_ref, new_field_any, sems.at[chunks])
+    field_out = pltpu.make_async_copy(field_ref, new_field_any, sems.at[1])
     field_out.start()
     sub = lax.broadcasted_iota(jnp.int32, (8, 128), 0)
     lane_c = lax.broadcasted_iota(jnp.int32, (CHUNK, 128), 1)
@@ -762,7 +759,6 @@
         -4.0 * point * (point - 1.0),
         2.0 * point * (point - 0.5),
     )
-    stores = []
     for c in range(chunks):
         rows = slice(c * CHUNK, (c + 1) * CHUNK)
         layer = planes[c * (CHUNK // 8) : (c + 1) * (CHUNK // 8), :]
@@ -782,11 +778,9 @@
         rate = under * (under * (gathered[rows, :] + side) + nucleation[rows, :])
         solid = solid_ref[rows, :]
         result[rows, :] = solid + (1.0 - solid) * (1.0 - jnp.exp(-rate))
-        copy = pltpu.make_async_copy(result.at[rows, :], new_solid_any.at[rows, :], sems.at[c])
+        copy = pltpu.make_async_copy(result.at[rows, :], new_solid_any.at[rows, :], sems.at[0])
         copy.start()
-        stores.append(copy)
-    for copy in stores:
-        copy.wait()
+    pltpu.make_async_copy(result, new_solid_any, sems.at[0]).wait()
     field_out.wait()
 
 
@@ -839,15 +833,15 @@
                 pltpu.VMEM((slabs, 2, 128), f32),
                 pltpu.VMEM((8, 128), f32),
                 pltpu.VMEM((8, 128), f32),
+                pltpu.SemaphoreType.DMA((7,)),
+                pltpu.SemaphoreType.DMA((4,)),
+                pltpu.SemaphoreType.DMA((2,)),
+                pltpu.SemaphoreType.DMA,
+                pltpu.SemaphoreType.REGULAR,
                 pltpu.SemaphoreType.DMA((9,)),
+                pltpu.SemaphoreType.DMA((2,)),
                 pltpu.SemaphoreType.DMA((4,)),
-                pltpu.SemaphoreType.DMA((5,)),
-                pltpu.SemaphoreType.DMA((3,)),
-                pltpu.SemaphoreType.REGULAR,
-                pltpu.SemaphoreType.DMA((4, 3)),
-                pltpu.SemaphoreType.DMA((4, 3)),
-                pltpu.SemaphoreType.DMA((4,)),
-                pltpu.SemaphoreType.DMA((4,)),
+                pltpu.SemaphoreType.DMA((2,)),
             ],
             compiler_params=pltpu.CompilerParams(
                 collective_id=0, has_side_effects=True, vmem_limit_bytes=16 << 20
@@ -878,7 +872,7 @@
             out_specs=(anywhere, anywhere),
             scratch_shapes=[
                 pltpu.VMEM(cells, f32),
-                pltpu.SemaphoreType.DMA((edge_x // CHUNK + 1,)),
+                pltpu.SemaphoreType.DMA((2,)),
             ],
             compiler_params=pltpu.CompilerParams(vmem_limit_bytes=16 << 20),
         )(*found)

time: 21.8 us -> 21.5 us (0.986)
    pallas_call x1, Pallas kernels: 20.1 us -> 19.9 us  [body(): pl.pallas_call(functools.partial(exchange, groups, slabs), out_shape=(jax...]
where the time goes in v5:
time: 21.5 us; the launch traced here: 21.4 us
  Pallas kernels  20.8 us (97%)
  between operations  0.64 us (3%)
    pallas_call x1, Pallas kernels, body(): pl.pallas_call(functools.partial(exchange, groups, slabs), out_shape=(jax...  19.9 us
    pallas_call x1, Pallas kernels, body(): pl.pallas_call(finish, out_shape=(jax.ShapeDtypeStruct(field.shape, f32),...  0.88 us

profile of v5, /device:TPU:1, one launch (start us, length us, event | category | flops | bytes accessed | tf_op | source)
XLA Modules:
  0.0 21.4 jit_solution(11842254870439479672)
XLA Ops:
  0.6 19.9 %shard_map.104 = (f32[2,512]{1,0:T(2,128)S(1)}, f32[512,128]{1,0:T(8,128)S(1)}, f32[72,384]{1,0:T(8,128)S(1)}, f32[512,128]{1,0:T(8,128)S(1)}, f32[512,128]{1,0:...) custom-call(f32[2,512]{1,0:T(2,128)} %field_any.1, f32[1,128]{1,0:T(1,128)} %kappa_any.1, f32[2,512]{1,0:T(2,128)} %heat_any.1, ...), custom_call_target="tpu_custom_call" | custom-call | tf_op jit(solution)/shard_map/pallas_call | solution.py:797
  20.5 0.9 %shard_map.105 = (f32[2,512]{1,0:T(2,128)}, f32[512,128]{1,0:T(8,128)}) custom-call(f32[2,512]{1,0:T(2,128)S(1)} %get-tuple-element.9.field_ref, f32[512,128]{1,0:T(8,128)S(1)} %get-tuple-element.10.solid_ref, f32[72,384]{1,0:T(8,128)S(1)} %get-tuple-element.11.planes, f32[512,128]{1,0:T(8,128)S(1)} %get-tuple-element.12.gathered, ...), custom_call_target="tpu_custom_call" | custom-call | tf_op jit(solution)/shard_map/pallas_call | solution.py:865

commit v6 on v5

--- a/solution.py
+++ b/solution.py
@@ -342,8 +342,24 @@
         greet(g, place(r))
         return carry
 
-    lax.fori_loop(0, jnp.where(ordered, 0, rank), greet_rank, 0)
-    lax.fori_loop(rank + 1, slabs, greet_rank, 0)
+    def greet_from(step, carry):
+        greet(g, (h + step) & (slabs - 1))
+        return carry
+
+    def greet_slab(to_h, carry):
+        greet(g, to_h)
+        return carry
+
+    first = ordered & sends_high
+    lax.fori_loop(28, jnp.where(ordered, 28, slabs), greet_from, 0)
+    lax.fori_loop(1, jnp.where(ordered, 1, 28), greet_from, 0)
+    lax.fori_loop(0, jnp.where(first, slabs - 2, 0), greet_slab, 0)
+
+    @pl.when(first & (rank == 0))
+    def _():
+        greet(g, jnp.int32(slabs - 1))
+
+    lax.fori_loop(jnp.where(ordered & jnp.logical_not(first), rank + 1, slabs), slabs, greet_rank, 0)
 
     wait_messages(8, load_sems.at[0])
     loads[2].wait()
@@ -377,8 +393,6 @@
     )
     for to_g, to_h, inside, upper in near_to.values():
         expected = expected + jnp.where(jnp.logical_not(inside | upper), 1, 0)
-
-    first = ordered & sends_high
 
     @pl.when(first)
     def _():

time: 21.5 us -> 21.2 us (0.986)
  Pallas kernels: 20.8 us -> 20.4 us
    pallas_call x1, Pallas kernels: 19.9 us -> 19.5 us  [body(): pl.pallas_call(functools.partial(exchange, groups, slabs), out_shape=(jax...]
where the time goes in v6:
time: 21.2 us; the launch traced here: 21 us
  Pallas kernels  20.4 us (96%)
  between operations  0.64 us (3%)
    pallas_call x1, Pallas kernels, body(): pl.pallas_call(functools.partial(exchange, groups, slabs), out_shape=(jax...  19.5 us
    pallas_call x1, Pallas kernels, body(): pl.pallas_call(finish, out_shape=(jax.ShapeDtypeStruct(field.shape, f32),...  0.88 us

profile of v6, /device:TPU:1, one launch (start us, length us, event | category | flops | bytes accessed | tf_op | source)
XLA Modules:
  0.0 21.0 jit_solution(809412864367844159)
XLA Ops:
  0.6 19.5 %shard_map.104 = (f32[2,512]{1,0:T(2,128)S(1)}, f32[512,128]{1,0:T(8,128)S(1)}, f32[72,384]{1,0:T(8,128)S(1)}, f32[512,128]{1,0:T(8,128)S(1)}, f32[512,128]{1,0:...) custom-call(f32[2,512]{1,0:T(2,128)} %field_any.1, f32[1,128]{1,0:T(1,128)} %kappa_any.1, f32[2,512]{1,0:T(2,128)} %heat_any.1, ...), custom_call_target="tpu_custom_call" | custom-call | tf_op jit(solution)/shard_map/pallas_call | solution.py:811
  20.1 0.9 %shard_map.105 = (f32[2,512]{1,0:T(2,128)}, f32[512,128]{1,0:T(8,128)}) custom-call(f32[2,512]{1,0:T(2,128)S(1)} %get-tuple-element.9.field_ref, f32[512,128]{1,0:T(8,128)S(1)} %get-tuple-element.10.solid_ref, f32[72,384]{1,0:T(8,128)S(1)} %get-tuple-element.11.planes, f32[512,128]{1,0:T(8,128)S(1)} %get-tuple-element.12.gathered, ...), custom_call_target="tpu_custom_call" | custom-call | tf_op jit(solution)/shard_map/pallas_call | solution.py:879
